TPU v7x, 768 devices: a whole 4x8x12 slice. The times are simulated.
768 devices in a mesh: gx: 24 (over z_hi, x, core), gy: 32 (over y, z_lo).
Axes of the slice: x: 4, y: 8, z: 12 (z_hi: 3, z_lo: 4; z = z_hi * 4 + z_lo), core: 2. Of those that a mesh axis runs over, the one named last changes fastest.
Arguments:
- populations: bfloat16 [2, 19, 384, 32768], P(None, None, 'gx', 'gy'), may hold values from 0 to 1, as said below
- wall_class: int32 [384, 32768], P('gx', 'gy'), may hold values from 0 to 3
- planes: int32 [2], replicated, may hold values from 0 to 383, as said below
Outputs:
- final_populations: bfloat16 [2, 19, 384, 32768], P(None, None, 'gx', 'gy')
Inputs may be any that keep to these rules, and one draw needn't show every extreme that they name: `populations`: every entry is positive. planes[0] lies below 96; planes[1] is the last x plane, 383.
All inputs are finite; a program needn't handle non-finite values.
Results may differ from a plain program's by a relative error of at most 0.0029.
Values may be sent and summed in bfloat16 or wider, within the bound.
A program may use at most 32 MiB of HBM per device.

v0:
```python
import jax
import jax.numpy as jnp
from jax import lax
from jax.sharding import PartitionSpec as P

NZ = 64
STEPS = 2


velocities = (
    (0, 0, 0),
    (1, 0, 0),
    (-1, 0, 0),
    (0, 1, 0),
    (0, -1, 0),
    (0, 0, 1),
    (0, 0, -1),
    (1, 1, 0),
    (-1, -1, 0),
    (1, -1, 0),
    (-1, 1, 0),
    (1, 0, 1),
    (-1, 0, -1),
    (1, 0, -1),
    (-1, 0, 1),
    (0, 1, 1),
    (0, -1, -1),
    (0, 1, -1),
    (0, -1, 1),
)
lattice_weights = (1.0 / 3.0,) + (1.0 / 18.0,) * 6 + (1.0 / 36.0,) * 12
COUPLING = 2.5
RELAX_TIMES = (1.0, 0.8)
STRENGTHS = (0.0, 0.15, 0.35, 0.6)
INLET_DENSITY = (1.0, 0.03)
OUTLET_DENSITY = (0.03, 1.0)
upward_x = (1, 7, 9, 11, 13)
downward_x = (2, 8, 10, 12, 14)
upward_y = (3, 7, 10, 15, 17)
downward_y = (4, 8, 9, 16, 18)


def padded(array, sides, width):
    for axis, dim in sides:
        size, length = (lax.axis_size(axis), array.shape[dim])
        up = [(i, (i + 1) % size) for i in range(size)]
        down = [(j, i) for i, j in up]
        last = lax.slice_in_dim(array, length - width, length, axis=dim)
        first = lax.slice_in_dim(array, 0, width, axis=dim)
        before = lax.ppermute(last, axis, up)
        after = lax.ppermute(first, axis, down)
        array = jnp.concatenate([before, array, after], axis=dim)
    return array


def passed_along(array, axis, by):
    size = lax.axis_size(axis)
    return lax.ppermute(array, axis, [(i, (i + by) % size) for i in range(size)])


def opposite(direction):
    if direction == 0:
        return 0
    return direction + 1 if direction % 2 == 1 else direction - 1


def wall_strength(wall_class):
    total = jnp.zeros(wall_class.shape, jnp.float32)
    for level in range(1, 4):
        total = total + jnp.where(
            wall_class == level, jnp.float32(STRENGTHS[level]), jnp.float32(0.0)
        )
    return total


def densities_of(pops):
    totals = []
    for component in range(2):
        total = pops[component, 0].astype(jnp.float32)
        for direction in range(1, 19):
            total = total + pops[component, direction].astype(jnp.float32)
        totals.append(total)
    return jnp.stack(totals)


def potential_of(densities, fluids):
    return jnp.where(fluids, 1.0 - jnp.exp(-densities), jnp.float32(0.0))


def directional_sum(field, lookup):
    totals = [None, None, None]
    for direction in range(1, 19):
        moved = lookup(field, velocities[direction])
        for axis_pos in range(3):
            along = velocities[direction][axis_pos]
            if along != 0:
                term = lattice_weights[direction] * along * moved
                totals[axis_pos] = term if totals[axis_pos] is None else totals[axis_pos] + term
    return totals


def interaction(potential_centre, pulls, wall_pulls):
    forces = []
    for component in range(2):
        partner = 1 - component
        wetting = 1.0 if component == 0 else -1.0
        forces.append(
            [
                -potential_centre[component]
                * (COUPLING * pulls[axis_pos][partner] + wetting * wall_pulls[axis_pos])
                for axis_pos in range(3)
            ]
        )
    return forces


def collide(pops, densities, forces, fluids):
    momenta = []
    for component in range(2):
        parts = []
        for axis_pos in range(3):
            total = jnp.zeros(densities.shape[1:], jnp.float32)
            for direction in range(1, 19):
                along = velocities[direction][axis_pos]
                if along != 0:
                    total = total + along * pops[component, direction].astype(jnp.float32)
            parts.append(total)
        momenta.append(parts)
    weight_sum = densities[0] / RELAX_TIMES[0] + densities[1] / RELAX_TIMES[1]
    common = [
        (momenta[0][axis_pos] / RELAX_TIMES[0] + momenta[1][axis_pos] / RELAX_TIMES[1]) / weight_sum
        for axis_pos in range(3)
    ]
    outputs = []
    for component in range(2):
        relax_time = RELAX_TIMES[component]
        velocity = [
            common[axis_pos] + relax_time * forces[component][axis_pos] / densities[component]
            for axis_pos in range(3)
        ]
        square = velocity[0] * velocity[0] + velocity[1] * velocity[1] + velocity[2] * velocity[2]
        for direction in range(19):
            vector = velocities[direction]
            along = vector[0] * velocity[0] + vector[1] * velocity[1] + vector[2] * velocity[2]
            equilibrium = (
                lattice_weights[direction]
                * densities[component]
                * (1.0 + 3.0 * along + 4.5 * along * along - 1.5 * square)
            )
            current = pops[component, direction].astype(jnp.float32)
            relaxed = current - (current - equilibrium) / relax_time
            bounced = pops[component, opposite(direction)]
            outputs.append(jnp.where(fluids, relaxed.astype(jnp.bfloat16), bounced))
    return jnp.stack(outputs).reshape((2, 19) + densities.shape[1:])


def stream(collided, lookup):
    outputs = []
    for component in range(2):
        for direction in range(19):
            vector = velocities[direction]
            outputs.append(
                lookup(collided[component, direction], (-vector[0], -vector[1], -vector[2]))
            )
    return jnp.stack(outputs).reshape((2, 19) + outputs[0].shape)


def reset(pops, xglobal, fluids, planes):
    at_inlet = jnp.logical_and(xglobal == planes[0], fluids)
    at_outlet = jnp.logical_and(xglobal == planes[1], fluids)
    outputs = []
    for component in range(2):
        for direction in range(19):
            inlet_value = jnp.asarray(
                lattice_weights[direction] * INLET_DENSITY[component], jnp.bfloat16
            )
            outlet_value = jnp.asarray(
                lattice_weights[direction] * OUTLET_DENSITY[component], jnp.bfloat16
            )
            outputs.append(
                jnp.where(
                    at_inlet,
                    inlet_value,
                    jnp.where(at_outlet, outlet_value, pops[component, direction]),
                )
            )
    return jnp.stack(outputs).reshape(pops.shape)


def z_move(field, step_z):
    if step_z == 0:
        return field
    lanes = field.shape[-1]
    zpos = lax.broadcasted_iota(jnp.int32, (lanes,), 0) % NZ
    if step_z == 1:
        inside = jnp.roll(field, -1, axis=-1)
        wrapped = jnp.roll(field, NZ - 1, axis=-1)
        return jnp.where(zpos == NZ - 1, wrapped, inside)
    inside = jnp.roll(field, 1, axis=-1)
    wrapped = jnp.roll(field, -(NZ - 1), axis=-1)
    return jnp.where(zpos == 0, wrapped, inside)


def pick(field, offset, vector, size_x, size_y):
    rank = field.ndim
    part_x = lax.slice_in_dim(field, offset + vector[0], offset + vector[0] + size_x, axis=rank - 2)
    start_y = (offset + vector[1]) * NZ
    part_y = lax.slice_in_dim(part_x, start_y, start_y + size_y * NZ, axis=rank - 1)
    return z_move(part_y, vector[2])


def widen_field(field, margin):
    grown = padded(field.astype(jnp.bfloat16), (("gx", 1),), margin).astype(field.dtype)
    return padded(grown.astype(jnp.bfloat16), (("gy", 2),), margin * NZ).astype(grown.dtype)


def place_rim(received, chosen, blank):
    rows = []
    for direction in range(19):
        if direction in chosen:
            rows.append(received[:, chosen.index(direction)])
        else:
            rows.append(blank)
    return jnp.stack(rows, axis=1)


def outgoing_faces(collided):
    lanes = collided.shape[3]
    upper_x = jnp.stack([collided[:, direction, -1:, :] for direction in upward_x], axis=1)
    lower_x = jnp.stack([collided[:, direction, :1, :] for direction in downward_x], axis=1)
    from_below = passed_along(upper_x, "gx", 1)
    from_above = passed_along(lower_x, "gx", -1)
    blank_x = jnp.zeros((2, 1, lanes), jnp.bfloat16)
    grown = jnp.concatenate(
        [
            place_rim(from_below, upward_x, blank_x),
            collided,
            place_rim(from_above, downward_x, blank_x),
        ],
        axis=2,
    )
    upper_y = jnp.stack([grown[:, direction, :, lanes - NZ :] for direction in upward_y], axis=1)
    lower_y = jnp.stack([grown[:, direction, :, :NZ] for direction in downward_y], axis=1)
    from_left = passed_along(upper_y, "gy", 1)
    from_right = passed_along(lower_y, "gy", -1)
    blank_y = jnp.zeros((2, grown.shape[2], NZ), jnp.bfloat16)
    return jnp.concatenate(
        [
            place_rim(from_left, upward_y, blank_y),
            grown,
            place_rim(from_right, downward_y, blank_y),
        ],
        axis=3,
    )


def on_device(populations, wall_class, planes):
    size_x = populations.shape[2]
    size_y = populations.shape[3] // NZ
    xglobal = (lax.axis_index("gx") * size_x + jnp.arange(size_x, dtype=jnp.int32)).reshape(
        size_x, 1
    )
    wall_wide = widen_field(wall_strength(wall_class)[None], 2)[0]
    fluids = wall_class == 0
    current = populations

    def inner_lookup(field, vector):
        return pick(field, 1, vector, size_x, size_y)

    def wall_lookup(field, vector):
        return pick(field, 2, vector, size_x, size_y)

    wall_pulls = directional_sum(wall_wide, wall_lookup)
    for repeat in range(STEPS):
        densities = densities_of(current)
        potential = potential_of(densities, fluids)
        potential_wide = widen_field(potential, 1)
        pulls = directional_sum(potential_wide, inner_lookup)
        forces = interaction(potential, pulls, wall_pulls)
        collided = collide(current, densities, forces, fluids)
        collided_wide = outgoing_faces(collided)
        read = stream(collided_wide, inner_lookup)
        current = reset(read, xglobal, fluids, planes)
    return current


def solution(mesh):
    in_specs = (P(None, None, "gx", "gy"), P("gx", "gy"), P())
    out_specs = P(None, None, "gx", "gy")
    return jax.shard_map(
        on_device, mesh=mesh, in_specs=in_specs, out_specs=out_specs, check_vma=False
    )
```

profile of v0, /device:TPU:7, one launch (start us, length us, event | category | flops | bytes accessed | tf_op | source)
XLA Modules:
  0.0 215.7 jit_solution(13600424512527984337)
XLA Ops:
  2.4 11.1 %collective-permute-start = (bf16[2,1,1024]{2,1,0:T(2,128)(2,1)S(1)}, bf16[2,1,1024]{2,1,0:T(2,128)(2,1)S(1)}, u32[]{:S(2)}, u32[]{:S(2)}) collective-permute-start(bf16[2,1,1024]{2,1,0:T(2,128)(2,1)S(1)} %get-tuple-element.275), channel_id=1, source_target_pairs={{0,32},{32,64},{64,96},{96,128},{128,160},{160,192},{192,224},{224... | collective-permute-start | bytes 12296 | tf_op jit(solution)/shard_map/ppermute | solution.py:50
  15.5 9.7 %collective-permute-start.4 = (bf16[1,2,1024]{2,1,0:T(2,128)(2,1)S(1)}, bf16[1,2,1024]{2,1,0:T(2,128)(2,1)S(1)}, u32[]{:S(2)}, u32[]{:S(2)}) collective-permute-start(bf16[1,2,1024]{2,1,0:T(2,128)(2,1)S(1)} %get-tuple-element.279), channel_id=1, source_target_pairs={{0,32},{32,64},{64,96},{96,128},{128,160},{160,192},{192,224},{224... | collective-permute-start | bytes 12296 | tf_op jit(solution)/shard_map/ppermute | solution.py:50
  25.2 1.9 collective-permute-start.5
  29.2 4.0 %collective-permute-start.2 = (bf16[2,18,64]{2,1,0:T(8,128)(2,1)S(1)}, bf16[2,18,64]{2,1,0:T(8,128)(2,1)S(1)}, u32[]{:S(2)}, u32[]{:S(2)}) collective-permute-start(bf16[2,18,64]{2,1,0:T(8,128)(2,1)S(1)} %get-tuple-element.232), channel_id=1, source_target_pairs={{0,1},{1,2},{2,3},{3,4},{4,5},{5,6},{6,7},{7,8},{8,9},{9,10},{10,1... | collective-permute-start | bytes 13832 | tf_op jit(solution)/shard_map/ppermute | solution.py:50
  33.2 8.1 %collective-permute-start.3 = (bf16[2,18,64]{2,1,0:T(8,128)(2,1)S(1)}, bf16[2,18,64]{2,1,0:T(8,128)(2,1)S(1)}, u32[]{:S(2)}, u32[]{:S(2)}) collective-permute-start(bf16[2,18,64]{2,1,0:T(8,128)(2,1)S(1)} %get-tuple-element.231), channel_id=1, source_target_pairs={{1,0},{2,1},{3,2},{4,3},{5,4},{6,5},{7,6},{8,7},{9,8},{10,9},{11,1... | collective-permute-start | bytes 13832 | tf_op jit(solution)/shard_map/ppermute | solution.py:51
  41.4 1.9 collective-permute-start.6
  43.3 7.3 %collective-permute-start.7 = (bf16[1,20,128]{2,1,0:T(8,128)(2,1)S(1)}, bf16[1,20,128]{2,1,0:T(8,128)(2,1)S(1)}, u32[]{:S(2)}, u32[]{:S(2)}) collective-permute-start(bf16[1,20,128]{2,1,0:T(8,128)(2,1)S(1)} %get-tuple-element.278), channel_id=1, source_target_pairs={{1,0},{2,1},{3,2},{4,3},{5,4},{6,5},{7,6},{8,7},{9,8},{10,9},{11,1... | collective-permute-start | bytes 15368 | tf_op jit(solution)/shard_map/ppermute | solution.py:51
  57.2 10.5 %collective-permute-start.8 = (bf16[2,5,1,1024]{3,0,2,1:T(2,128)(2,1)S(1)}, bf16[2,5,1,1024]{3,0,2,1:T(2,128)(2,1)S(1)}, u32[]{:S(2)}, u32[]{:S(2)}) collective-permute-start(bf16[2,5,1,1024]{3,0,2,1:T(2,128)(2,1)S(1)} %constant_dynamic-update-slice_fusion.38), channel_id=1, source_target_pairs={{0,32},{32,64},{64,96},{96,128},{128,160},{160,192},{192,224},{224... | collective-permute-start | bytes 61448 | tf_op jit(solution)/shard_map/ppermute | solution.py:58
  71.2 9.0 %collective-permute-done.9 = bf16[2,5,1,1024]{3,0,2,1:T(2,128)(2,1)S(1)} collective-permute-done((bf16[2,5,1,1024]{3,0,2,1:T(2,128)(2,1)S(1)}, bf16[2,5,1,1024]{3,0,2,1:T(2,128)(2,1)S(1)}, u32[]{:S(2)}, u32[]{:S(2)}) %collective-permute-start.9) | collective-permute-done | bytes 20512 | tf_op jit(solution)/shard_map/ppermute | solution.py:58
  80.4 3.4 %pad_maximum_fusion = bf16[2,19,18,1024]{3,0,2,1:T(2,128)(2,1)S(1)} fusion(bf16[2,19,1,1024]{3,0,2,1:T(2,128)(2,1)S(1)} %constant_dynamic-update-slice_fusion.61, bf16[2,19,16,1024]{3,0,2,1:T(2,128)(2,1)S(1)} %copy.78, bf16[2,19,1,1024]{3,0,2,1:T(2,128)(2,1)S(1)} %constant_dynamic-update-slice_fusion.43), kind=kLoop, calls=%fused_computation | loop fusion | flops 1400832 | bytes 2801664 | tf_op jit(solution)/shard_map/concatenate | solution.py:234
  84.3 7.2 %collective-permute-start.11 = (bf16[2,5,18,64]{3,0,2,1:T(2,128)(2,1)S(1)}, bf16[2,5,18,64]{3,0,2,1:T(2,128)(2,1)S(1)}, u32[]{:S(2)}, u32[]{:S(2)}) collective-permute-start(bf16[2,5,18,64]{3,0,2,1:T(2,128)(2,1)S(1)} %pad_maximum_fusion.4), channel_id=1, source_target_pairs={{0,31},{1,0},{2,1},{3,2},{4,3},{5,4},{6,5},{7,6},{8,7},{9,8},{10,9... | collective-permute-start | bytes 69128 | tf_op jit(solution)/shard_map/ppermute | solution.py:58
  92.8 2.1 collective-permute-start.10
  95.1 6.4 %collective-permute-done.10 = bf16[2,5,18,64]{3,0,2,1:T(2,128)(2,1)S(1)} collective-permute-done((bf16[2,5,18,64]{3,0,2,1:T(2,128)(2,1)S(1)}, bf16[2,5,18,64]{3,0,2,1:T(2,128)(2,1)S(1)}, u32[]{:S(2)}, u32[]{:S(2)}) %collective-permute-start.10) | collective-permute-done | bytes 23072 | tf_op jit(solution)/shard_map/ppermute | solution.py:58
  102.4 9.2 %concatenate.1395 = bf16[2,19,18,1152]{3,0,2,1:T(2,128)(2,1)S(1)} concatenate(bf16[2,19,18,64]{3,0,2,1:T(2,128)(2,1)} %copy-done.4, bf16[2,19,18,1024]{3,0,2,1:T(2,128)(2,1)S(1)} %pad_maximum_fusion, bf16[2,19,18,64]{3,0,2,1:T(2,128)(2,1)S(1)} %constant_dynamic-update-slice_fusion.91), dimensions={3} | concatenate | bytes 3151872 | tf_op jit(solution)/shard_map/concatenate | solution.py:247
  126.0 3.4 %collective-permute-start.12 = (bf16[2,1,1024]{2,1,0:T(2,128)(2,1)S(1)}, bf16[2,1,1024]{2,1,0:T(2,128)(2,1)S(1)}, u32[]{:S(2)}, u32[]{:S(2)}) collective-permute-start(bf16[2,1,1024]{2,1,0:T(2,128)(2,1)S(1)} %get-tuple-element.273), channel_id=1, source_target_pairs={{0,32},{32,64},{64,96},{96,128},{128,160},{160,192},{192,224},{224... | collective-permute-start | bytes 12296 | tf_op jit(solution)/shard_map/ppermute | solution.py:50
  131.3 9.0 %collective-permute-done.13 = bf16[2,1,1024]{2,1,0:T(2,128)(2,1)S(1)} collective-permute-done((bf16[2,1,1024]{2,1,0:T(2,128)(2,1)S(1)}, bf16[2,1,1024]{2,1,0:T(2,128)(2,1)S(1)}, u32[]{:S(2)}, u32[]{:S(2)}) %collective-permute-start.13) | collective-permute-done | bytes 4128 | tf_op jit(solution)/shard_map/ppermute | solution.py:51
  142.4 7.5 %collective-permute-start.15 = (bf16[2,18,64]{2,1,0:T(8,128)(2,1)S(1)}, bf16[2,18,64]{2,1,0:T(8,128)(2,1)S(1)}, u32[]{:S(2)}, u32[]{:S(2)}) collective-permute-start(bf16[2,18,64]{2,1,0:T(8,128)(2,1)S(1)} %get-tuple-element.229), channel_id=1, source_target_pairs={{1,0},{2,1},{3,2},{4,3},{5,4},{6,5},{7,6},{8,7},{9,8},{10,9},{11,1... | collective-permute-start | bytes 13832 | tf_op jit(solution)/shard_map/ppermute | solution.py:51
  155.3 3.1 %collective-permute-start.16 = (bf16[2,5,1,1024]{3,0,2,1:T(2,128)(2,1)S(1)}, bf16[2,5,1,1024]{3,0,2,1:T(2,128)(2,1)S(1)}, u32[]{:S(2)}, u32[]{:S(2)}) collective-permute-start(bf16[2,5,1,1024]{3,0,2,1:T(2,128)(2,1)S(1)} %constant_dynamic-update-slice_fusion.215), channel_id=1, source_target_pairs={{0,32},{32,64},{64,96},{96,128},{128,160},{160,192},{192,224},{224... | collective-permute-start | bytes 61448 | tf_op jit(solution)/shard_map/ppermute | solution.py:58
  161.8 9.0 %collective-permute-done.17 = bf16[2,5,1,1024]{3,0,2,1:T(2,128)(2,1)S(1)} collective-permute-done((bf16[2,5,1,1024]{3,0,2,1:T(2,128)(2,1)S(1)}, bf16[2,5,1,1024]{3,0,2,1:T(2,128)(2,1)S(1)}, u32[]{:S(2)}, u32[]{:S(2)}) %collective-permute-start.17) | collective-permute-done | bytes 20512 | tf_op jit(solution)/shard_map/ppermute | solution.py:58
  171.0 3.4 %pad_maximum_fusion.1 = bf16[2,19,18,1024]{3,0,2,1:T(2,128)(2,1)S(1)} fusion(bf16[2,19,1,1024]{3,0,2,1:T(2,128)(2,1)S(1)} %constant_dynamic-update-slice_fusion.238, bf16[2,19,16,1024]{3,0,2,1:T(2,128)(2,1)S(1)} %copy.147, bf16[2,19,1,1024]{3,0,2,1:T(2,128)(2,1)S(1)} %constant_dynamic-update-slice_fusion.220), kind=kLoop, calls=%fused_computation.1 | loop fusion | flops 1400832 | bytes 2801664 | tf_op jit(solution)/shard_map/concatenate | solution.py:234
  175.0 7.8 %collective-permute-start.19 = (bf16[2,5,18,64]{3,0,2,1:T(2,128)(2,1)S(1)}, bf16[2,5,18,64]{3,0,2,1:T(2,128)(2,1)S(1)}, u32[]{:S(2)}, u32[]{:S(2)}) collective-permute-start(bf16[2,5,18,64]{3,0,2,1:T(2,128)(2,1)S(1)} %pad_maximum_fusion.5), channel_id=1, source_target_pairs={{0,31},{1,0},{2,1},{3,2},{4,3},{5,4},{6,5},{7,6},{8,7},{9,8},{10,9... | collective-permute-start | bytes 69128 | tf_op jit(solution)/shard_map/ppermute | solution.py:58
  182.8 2.2 %collective-permute-start.18 = (bf16[2,5,18,64]{3,0,2,1:T(2,128)(2,1)S(1)}, bf16[2,5,18,64]{3,0,2,1:T(2,128)(2,1)S(1)}, u32[]{:S(2)}, u32[]{:S(2)}) collective-permute-start(bf16[2,5,18,64]{3,0,2,1:T(2,128)(2,1)S(1)} %get-tuple-element.121), channel_id=1, source_target_pairs={{0,1},{1,2},{2,3},{3,4},{4,5},{5,6},{6,7},{7,8},{8,9},{9,10},{10,1... | collective-permute-start | bytes 69128 | tf_op jit(solution)/shard_map/ppermute | solution.py:58
  185.2 6.3 %collective-permute-done.18 = bf16[2,5,18,64]{3,0,2,1:T(2,128)(2,1)S(1)} collective-permute-done((bf16[2,5,18,64]{3,0,2,1:T(2,128)(2,1)S(1)}, bf16[2,5,18,64]{3,0,2,1:T(2,128)(2,1)S(1)}, u32[]{:S(2)}, u32[]{:S(2)}) %collective-permute-start.18) | collective-permute-done | bytes 23072 | tf_op jit(solution)/shard_map/ppermute | solution.py:58
  191.8 8.7 %concatenate.1539 = bf16[2,19,18,1152]{3,0,2,1:T(2,128)(2,1)S(1)} concatenate(bf16[2,19,18,64]{3,0,2,1:T(2,128)(2,1)S(1)} %constant_dynamic-update-slice_fusion.255, bf16[2,19,18,1024]{3,0,2,1:T(2,128)(2,1)S(1)} %pad_maximum_fusion.1, bf16[2,19,18,64]{3,0,2,1:T(2,128)(2,1)S(1)} %constant_dynamic-update-slice_fusion.268), dimensions={3} | concatenate | bytes 3151872 | tf_op jit(solution)/shard_map/concatenate | solution.py:247
  (683 shorter events, 60.9 us)
Async XLA Ops:
  0.0 2.3 %copy-start = (s32[16,1024]{1,0:T(8,128)S(1)}, s32[16,1024]{1,0:T(8,128)}, u32[]{:S(2)}) copy-start(s32[16,1024]{1,0:T(8,128)} %param.4) | copy-start | bytes 196612
  0.0 28.4 %copy-start.5 = (s32[2]{0:T(128)S(1)}, s32[2]{0:T(128)}, u32[]{:S(2)}) copy-start(s32[2]{0:T(128)} %param.5) | copy-start | bytes 28
  2.4 26.6 %collective-permute-start = (bf16[2,1,1024]{2,1,0:T(2,128)(2,1)S(1)}, bf16[2,1,1024]{2,1,0:T(2,128)(2,1)S(1)}, u32[]{:S(2)}, u32[]{:S(2)}) collective-permute-start(bf16[2,1,1024]{2,1,0:T(2,128)(2,1)S(1)} %get-tuple-element.275), channel_id=1, source_target_pairs={{0,32},{32,64},{64,96},{96,128},{128,160},{160,192},{192,224},{224... | collective-permute-start | bytes 12296 | tf_op jit(solution)/shard_map/ppermute | solution.py:50
  13.5 15.5 %collective-permute-start.1 = (bf16[2,1,1024]{2,1,0:T(2,128)(2,1)S(1)}, bf16[2,1,1024]{2,1,0:T(2,128)(2,1)S(1)}, u32[]{:S(2)}, u32[]{:S(2)}) collective-permute-start(bf16[2,1,1024]{2,1,0:T(2,128)(2,1)S(1)} %get-tuple-element.276), channel_id=1, source_target_pairs={{32,0},{64,32},{96,64},{128,96},{160,128},{192,160},{224,192},{256... | collective-permute-start | bytes 12296 | tf_op jit(solution)/shard_map/ppermute | solution.py:51
  15.5 25.8 %collective-permute-start.4 = (bf16[1,2,1024]{2,1,0:T(2,128)(2,1)S(1)}, bf16[1,2,1024]{2,1,0:T(2,128)(2,1)S(1)}, u32[]{:S(2)}, u32[]{:S(2)}) collective-permute-start(bf16[1,2,1024]{2,1,0:T(2,128)(2,1)S(1)} %get-tuple-element.279), channel_id=1, source_target_pairs={{0,32},{32,64},{64,96},{96,128},{128,160},{160,192},{192,224},{224... | collective-permute-start | bytes 12296 | tf_op jit(solution)/shard_map/ppermute | solution.py:50
  25.2 16.2 %collective-permute-start.5 = (bf16[1,2,1024]{2,1,0:T(2,128)(2,1)S(1)}, bf16[1,2,1024]{2,1,0:T(2,128)(2,1)S(1)}, u32[]{:S(2)}, u32[]{:S(2)}) collective-permute-start(bf16[1,2,1024]{2,1,0:T(2,128)(2,1)S(1)} %get-tuple-element.280), channel_id=1, source_target_pairs={{32,0},{64,32},{96,64},{128,96},{160,128},{192,160},{224,192},{256... | collective-permute-start | bytes 12296 | tf_op jit(solution)/shard_map/ppermute | solution.py:51
  29.2 21.4 %collective-permute-start.2 = (bf16[2,18,64]{2,1,0:T(8,128)(2,1)S(1)}, bf16[2,18,64]{2,1,0:T(8,128)(2,1)S(1)}, u32[]{:S(2)}, u32[]{:S(2)}) collective-permute-start(bf16[2,18,64]{2,1,0:T(8,128)(2,1)S(1)} %get-tuple-element.232), channel_id=1, source_target_pairs={{0,1},{1,2},{2,3},{3,4},{4,5},{5,6},{6,7},{7,8},{8,9},{9,10},{10,1... | collective-permute-start | bytes 13832 | tf_op jit(solution)/shard_map/ppermute | solution.py:50
  33.2 17.4 %collective-permute-start.3 = (bf16[2,18,64]{2,1,0:T(8,128)(2,1)S(1)}, bf16[2,18,64]{2,1,0:T(8,128)(2,1)S(1)}, u32[]{:S(2)}, u32[]{:S(2)}) collective-permute-start(bf16[2,18,64]{2,1,0:T(8,128)(2,1)S(1)} %get-tuple-element.231), channel_id=1, source_target_pairs={{1,0},{2,1},{3,2},{4,3},{5,4},{6,5},{7,6},{8,7},{9,8},{10,9},{11,1... | collective-permute-start | bytes 13832 | tf_op jit(solution)/shard_map/ppermute | solution.py:51
  41.4 11.1 %collective-permute-start.6 = (bf16[1,20,128]{2,1,0:T(8,128)(2,1)S(1)}, bf16[1,20,128]{2,1,0:T(8,128)(2,1)S(1)}, u32[]{:S(2)}, u32[]{:S(2)}) collective-permute-start(bf16[1,20,128]{2,1,0:T(8,128)(2,1)S(1)} %get-tuple-element.277), channel_id=1, source_target_pairs={{0,1},{1,2},{2,3},{3,4},{4,5},{5,6},{6,7},{7,8},{8,9},{9,10},{10,1... | collective-permute-start | bytes 15368 | tf_op jit(solution)/shard_map/ppermute | solution.py:50
  43.3 9.2 %collective-permute-start.7 = (bf16[1,20,128]{2,1,0:T(8,128)(2,1)S(1)}, bf16[1,20,128]{2,1,0:T(8,128)(2,1)S(1)}, u32[]{:S(2)}, u32[]{:S(2)}) collective-permute-start(bf16[1,20,128]{2,1,0:T(8,128)(2,1)S(1)} %get-tuple-element.278), channel_id=1, source_target_pairs={{1,0},{2,1},{3,2},{4,3},{5,4},{6,5},{7,6},{8,7},{9,8},{10,9},{11,1... | collective-permute-start | bytes 15368 | tf_op jit(solution)/shard_map/ppermute | solution.py:51
  57.2 13.8 %collective-permute-start.8 = (bf16[2,5,1,1024]{3,0,2,1:T(2,128)(2,1)S(1)}, bf16[2,5,1,1024]{3,0,2,1:T(2,128)(2,1)S(1)}, u32[]{:S(2)}, u32[]{:S(2)}) collective-permute-start(bf16[2,5,1,1024]{3,0,2,1:T(2,128)(2,1)S(1)} %constant_dynamic-update-slice_fusion.38), channel_id=1, source_target_pairs={{0,32},{32,64},{64,96},{96,128},{128,160},{160,192},{192,224},{224... | collective-permute-start | bytes 61448 | tf_op jit(solution)/shard_map/ppermute | solution.py:58
  69.1 11.1 %collective-permute-start.9 = (bf16[2,5,1,1024]{3,0,2,1:T(2,128)(2,1)S(1)}, bf16[2,5,1,1024]{3,0,2,1:T(2,128)(2,1)S(1)}, u32[]{:S(2)}, u32[]{:S(2)}) collective-permute-start(bf16[2,5,1,1024]{3,0,2,1:T(2,128)(2,1)S(1)} %constant_dynamic-update-slice_fusion.56), channel_id=1, source_target_pairs={{0,736},{32,0},{64,32},{96,64},{128,96},{160,128},{192,160},{224,1... | collective-permute-start | bytes 61448 | tf_op jit(solution)/shard_map/ppermute | solution.py:58
  84.3 10.6 %collective-permute-start.11 = (bf16[2,5,18,64]{3,0,2,1:T(2,128)(2,1)S(1)}, bf16[2,5,18,64]{3,0,2,1:T(2,128)(2,1)S(1)}, u32[]{:S(2)}, u32[]{:S(2)}) collective-permute-start(bf16[2,5,18,64]{3,0,2,1:T(2,128)(2,1)S(1)} %pad_maximum_fusion.4), channel_id=1, source_target_pairs={{0,31},{1,0},{2,1},{3,2},{4,3},{5,4},{6,5},{7,6},{8,7},{9,8},{10,9... | collective-permute-start | bytes 69128 | tf_op jit(solution)/shard_map/ppermute | solution.py:58
  92.8 8.7 %collective-permute-start.10 = (bf16[2,5,18,64]{3,0,2,1:T(2,128)(2,1)S(1)}, bf16[2,5,18,64]{3,0,2,1:T(2,128)(2,1)S(1)}, u32[]{:S(2)}, u32[]{:S(2)}) collective-permute-start(bf16[2,5,18,64]{3,0,2,1:T(2,128)(2,1)S(1)} %get-tuple-element.125), channel_id=1, source_target_pairs={{0,1},{1,2},{2,3},{3,4},{4,5},{5,6},{6,7},{7,8},{8,9},{9,10},{10,1... | collective-permute-start | bytes 69128 | tf_op jit(solution)/shard_map/ppermute | solution.py:58
  126.0 5.3 %collective-permute-start.12 = (bf16[2,1,1024]{2,1,0:T(2,128)(2,1)S(1)}, bf16[2,1,1024]{2,1,0:T(2,128)(2,1)S(1)}, u32[]{:S(2)}, u32[]{:S(2)}) collective-permute-start(bf16[2,1,1024]{2,1,0:T(2,128)(2,1)S(1)} %get-tuple-element.273), channel_id=1, source_target_pairs={{0,32},{32,64},{64,96},{96,128},{128,160},{160,192},{192,224},{224... | collective-permute-start | bytes 12296 | tf_op jit(solution)/shard_map/ppermute | solution.py:50
  129.4 11.0 %collective-permute-start.13 = (bf16[2,1,1024]{2,1,0:T(2,128)(2,1)S(1)}, bf16[2,1,1024]{2,1,0:T(2,128)(2,1)S(1)}, u32[]{:S(2)}, u32[]{:S(2)}) collective-permute-start(bf16[2,1,1024]{2,1,0:T(2,128)(2,1)S(1)} %get-tuple-element.274), channel_id=1, source_target_pairs={{32,0},{64,32},{96,64},{128,96},{160,128},{192,160},{224,192},{256... | collective-permute-start | bytes 12296 | tf_op jit(solution)/shard_map/ppermute | solution.py:51
  140.5 9.4 %collective-permute-start.14 = (bf16[2,18,64]{2,1,0:T(8,128)(2,1)S(1)}, bf16[2,18,64]{2,1,0:T(8,128)(2,1)S(1)}, u32[]{:S(2)}, u32[]{:S(2)}) collective-permute-start(bf16[2,18,64]{2,1,0:T(8,128)(2,1)S(1)} %get-tuple-element.230), channel_id=1, source_target_pairs={{0,1},{1,2},{2,3},{3,4},{4,5},{5,6},{6,7},{7,8},{8,9},{9,10},{10,1... | collective-permute-start | bytes 13832 | tf_op jit(solution)/shard_map/ppermute | solution.py:50
  142.4 8.1 %collective-permute-start.15 = (bf16[2,18,64]{2,1,0:T(8,128)(2,1)S(1)}, bf16[2,18,64]{2,1,0:T(8,128)(2,1)S(1)}, u32[]{:S(2)}, u32[]{:S(2)}) collective-permute-start(bf16[2,18,64]{2,1,0:T(8,128)(2,1)S(1)} %get-tuple-element.229), channel_id=1, source_target_pairs={{1,0},{2,1},{3,2},{4,3},{5,4},{6,5},{7,6},{8,7},{9,8},{10,9},{11,1... | collective-permute-start | bytes 13832 | tf_op jit(solution)/shard_map/ppermute | solution.py:51
  155.3 6.4 %collective-permute-start.16 = (bf16[2,5,1,1024]{3,0,2,1:T(2,128)(2,1)S(1)}, bf16[2,5,1,1024]{3,0,2,1:T(2,128)(2,1)S(1)}, u32[]{:S(2)}, u32[]{:S(2)}) collective-permute-start(bf16[2,5,1,1024]{3,0,2,1:T(2,128)(2,1)S(1)} %constant_dynamic-update-slice_fusion.215), channel_id=1, source_target_pairs={{0,32},{32,64},{64,96},{96,128},{128,160},{160,192},{192,224},{224... | collective-permute-start | bytes 61448 | tf_op jit(solution)/shard_map/ppermute | solution.py:58
  159.7 11.1 %collective-permute-start.17 = (bf16[2,5,1,1024]{3,0,2,1:T(2,128)(2,1)S(1)}, bf16[2,5,1,1024]{3,0,2,1:T(2,128)(2,1)S(1)}, u32[]{:S(2)}, u32[]{:S(2)}) collective-permute-start(bf16[2,5,1,1024]{3,0,2,1:T(2,128)(2,1)S(1)} %constant_dynamic-update-slice_fusion.233), channel_id=1, source_target_pairs={{0,736},{32,0},{64,32},{96,64},{128,96},{160,128},{192,160},{224,1... | collective-permute-start | bytes 61448 | tf_op jit(solution)/shard_map/ppermute | solution.py:58
  171.0 11.8 %copy-start.3 = (bf16[2,19,18,64]{3,0,2,1:T(2,128)(2,1)S(1)}, bf16[2,19,18,64]{3,0,2,1:T(2,128)(2,1)}, u32[]{:S(2)}) copy-start(bf16[2,19,18,64]{3,0,2,1:T(2,128)(2,1)} %constant_dynamic-update-slice_fusion.267) | copy-start | bytes 262660
  171.0 14.0 %copy-start.2 = (bf16[2,19,18,64]{3,0,2,1:T(2,128)(2,1)S(1)}, bf16[2,19,18,64]{3,0,2,1:T(2,128)(2,1)}, u32[]{:S(2)}) copy-start(bf16[2,19,18,64]{3,0,2,1:T(2,128)(2,1)} %constant_dynamic-update-slice_fusion.277) | copy-start | bytes 262660
  175.0 10.1 %collective-permute-start.19 = (bf16[2,5,18,64]{3,0,2,1:T(2,128)(2,1)S(1)}, bf16[2,5,18,64]{3,0,2,1:T(2,128)(2,1)S(1)}, u32[]{:S(2)}, u32[]{:S(2)}) collective-permute-start(bf16[2,5,18,64]{3,0,2,1:T(2,128)(2,1)S(1)} %pad_maximum_fusion.5), channel_id=1, source_target_pairs={{0,31},{1,0},{2,1},{3,2},{4,3},{5,4},{6,5},{7,6},{8,7},{9,8},{10,9... | collective-permute-start | bytes 69128 | tf_op jit(solution)/shard_map/ppermute | solution.py:58
  182.8 8.7 %collective-permute-start.18 = (bf16[2,5,18,64]{3,0,2,1:T(2,128)(2,1)S(1)}, bf16[2,5,18,64]{3,0,2,1:T(2,128)(2,1)S(1)}, u32[]{:S(2)}, u32[]{:S(2)}) collective-permute-start(bf16[2,5,18,64]{3,0,2,1:T(2,128)(2,1)S(1)} %get-tuple-element.121), channel_id=1, source_target_pairs={{0,1},{1,2},{2,3},{3,4},{4,5},{5,6},{6,7},{7,8},{8,9},{9,10},{10,1... | collective-permute-start | bytes 69128 | tf_op jit(solution)/shard_map/ppermute | solution.py:58
  (3 other events, 3.0 us)
where the time goes:
time: 217 us; the launch traced here: 216 us
  starting transfers between devices  97.3 us (45%)
  local copies, waits for them, and re-layouts  46.6 us (21%)
  waiting for transfers between devices  40.4 us (19%)
  other arithmetic  28.7 us (13%)
  between operations  2.69 us (1%)
    ppermute x8, starting transfers between devices, passed_along(): lax.ppermute(array, axis, [(i, (i + by) % size) for i in range(size)])  36.7 us
    ppermute x6, starting transfers between devices, padded(): before = lax.ppermute(last, axis, up)  31.9 us
    ppermute x8, waiting for transfers between devices, passed_along(): lax.ppermute(array, axis, [(i, (i + by) % size) for i in range(size)])  30.7 us
    ppermute x6, starting transfers between devices, padded(): after = lax.ppermute(first, axis, down)  28.7 us
    concatenate x2, local copies, waits for them, and re-layouts, outgoing_faces(): jnp.concatenate([place_rim(from_left, upward_y, blank_y), grown, place_ri...  17.9 us
    unnamed x186, other arithmetic  15.3 us
    ppermute x6, waiting for transfers between devices, padded(): after = lax.ppermute(first, axis, down)  9.61 us
    unnamed x238, local copies, waits for them, and re-layouts  7.32 us
  transfers between devices with their start and end apart: 20, of which 6 were waited for; matrix products, arithmetic and copies ran while one was open for 4% of the time, Pallas kernels for 0%

commit v1 on v0

v1 whole, which is shorter than its diff:
```python
import functools

import jax
import jax.numpy as jnp
import numpy as np
from jax import lax
from jax.experimental import pallas as pl
from jax.experimental.pallas import tpu as pltpu
from jax.sharding import PartitionSpec as P

NZ = 64
STEPS = 2
MESH = pl.DeviceIdType.MESH
velocities = (
    (0, 0, 0),
    (1, 0, 0),
    (-1, 0, 0),
    (0, 1, 0),
    (0, -1, 0),
    (0, 0, 1),
    (0, 0, -1),
    (1, 1, 0),
    (-1, -1, 0),
    (1, -1, 0),
    (-1, 1, 0),
    (1, 0, 1),
    (-1, 0, -1),
    (1, 0, -1),
    (-1, 0, 1),
    (0, 1, 1),
    (0, -1, -1),
    (0, 1, -1),
    (0, -1, 1),
)
lattice_weights = (1.0 / 3.0,) + (1.0 / 18.0,) * 6 + (1.0 / 36.0,) * 12
COUPLING = 2.5
RELAX_TIMES = (1.0, 0.8)
STRENGTHS = (0.0, 0.15, 0.35, 0.6)
INLET_DENSITY = (1.0, 0.03)
OUTLET_DENSITY = (0.03, 1.0)
along_x = ((1, 7, 9, 11, 13), (2, 8, 10, 12, 14))
along_y = ((3, 7, 10, 15, 17), (4, 8, 9, 16, 18))
along_edge = {(0, 0): 7, (1, 1): 8, (0, 1): 9, (1, 0): 10}
EDGES = ((0, 0), (0, 1), (1, 0), (1, 1))

HALO = 8


def opposite(direction):
    if direction == 0:
        return 0
    return direction + 1 if direction % 2 == 1 else direction - 1


def kernel(
    nx_devices,
    ny_devices,
    pops_hbm,
    wall_ref,
    planes_ref,
    out_ref,
    pops,
    field,
    spread,
    aux,
    stream,
    pot_sx,
    pot_sy,
    pot_rx,
    pot_ry,
    pot_rc,
    pop_sx,
    pop_sy,
    pop_rx,
    pop_ry,
    pop_rc,
    in_sem,
    send_sem,
    recv_sem,
):
    size_x = pops.shape[2]
    tiles = pops.shape[3] // 128
    halves = size_x // 8
    rows = size_x + 2 * HALO
    block = (tiles + 2) * rows
    f32 = jnp.float32
    bf16 = jnp.bfloat16

    gx = lax.axis_index("gx")
    gy = lax.axis_index("gy")
    near_x = (lax.rem(gx + 1, nx_devices), lax.rem(gx + nx_devices - 1, nx_devices))
    near_y = (lax.rem(gy + 1, ny_devices), lax.rem(gy + ny_devices - 1, ny_devices))

    def load_in(t):
        lanes = pl.ds(pl.multiple_of(t * 128, 128), 128)
        return pltpu.make_async_copy(
            pops_hbm.at[:, :, :, lanes], pops.at[:, :, :, lanes], in_sem.at[t]
        )

    for t in range(tiles):
        load_in(t).start()

    barrier = pltpu.get_barrier_semaphore()
    targets = [(near_x[0], gy), (near_x[1], gy), (gx, near_y[0]), (gx, near_y[1])]
    targets += [(near_x[i], near_y[j]) for i, j in EDGES]
    for target in targets:
        pl.semaphore_signal(barrier, inc=1, device_id=target, device_id_type=MESH)

    lane = lax.broadcasted_iota(jnp.int32, (8, 128), 1)
    row_index = lax.broadcasted_iota(jnp.int32, (8, 128), 0)
    low = lane < NZ
    first_z = jnp.logical_or(lane == 0, lane == NZ)
    last_z = jnp.logical_or(lane == NZ - 1, lane == 2 * NZ - 1)

    def roll(value, by):
        return pltpu.roll(value, by % 128, 1)

    def z_from_below(value, turned):
        return roll(jnp.where(last_z, turned, value), 1)

    def z_from_above(value, turned):
        return roll(jnp.where(first_z, turned, value), -1)

    def at(index, tile, row):
        return pl.ds(pl.multiple_of(index * block + tile * rows + row, 8), 8)

    def off(index, tile, row):
        return pl.ds(index * block + tile * rows + row, 8)

    def across(index, row):
        return pl.ds(index * block + rows + row, tiles, stride=rows)

    def spot(t, half):
        return pl.ds(pl.multiple_of(t * size_x + half * 8, 8), 8)

    def fluid_at(t, half):
        lanes = pl.ds(pl.multiple_of(t * 128, 128), 128)
        return wall_ref[half * 8 : half * 8 + 8, lanes]

    def pop_at(component, direction, t, half):
        lanes = pl.ds(pl.multiple_of(t * 128, 128), 128)
        return pops[component, direction, half * 8 : half * 8 + 8, lanes].astype(f32)

    def store_potential(t, half, densities):
        wall = fluid_at(t, half)
        fluid = wall == 0
        strength = jnp.where(
            wall == 1, STRENGTHS[1], jnp.where(wall == 2, STRENGTHS[2], STRENGTHS[3])
        )
        oil = COUPLING * (1.0 - jnp.exp(-densities[0]))
        brine = COUPLING * (1.0 - jnp.exp(-densities[1]))
        field[at(0, t + 1, HALO + half * 8), :] = jnp.where(fluid, brine, strength)
        field[at(1, t + 1, HALO + half * 8), :] = jnp.where(fluid, oil, -strength)
        aux[0, spot(t, half), :] = densities[0]
        aux[1, spot(t, half), :] = densities[1]

    def first_density(t, carry):
        load_in(t).wait()
        for half in range(halves):
            densities = []
            for component in range(2):
                total = pop_at(component, 0, t, half)
                for direction in range(1, 19):
                    total = total + pop_at(component, direction, t, half)
                densities.append(total)
            store_potential(t, half, densities)
        return carry

    def exchange(number, sends_x, sends_y, edge_source, recvs_x, recvs_y, recvs_c):
        copies = []
        for side in range(2):
            copies.append((sends_x.at[side], recvs_x.at[side], (near_x[side], gy)))
            copies.append((sends_y.at[side], recvs_y.at[side], (gx, near_y[side])))
        for place, (i, j) in enumerate(EDGES):
            copies.append((edge_source(i, j), recvs_c.at[place], (near_x[i], near_y[j])))
        started = []
        for place, (source, target, device) in enumerate(copies):
            copy = pltpu.make_async_remote_copy(
                src_ref=source,
                dst_ref=target,
                send_sem=send_sem.at[number, place],
                recv_sem=recv_sem.at[number, place],
                device_id=device,
                device_id_type=MESH,
            )
            copy.start()
            started.append(copy)
        return started

    def send_potential(step):
        for side in range(2):
            row = HALO + size_x - 1 if side == 0 else HALO
            tile = tiles if side == 0 else 1
            for index in range(2):
                pot_sx[step, side, index] = field[across(index, row), :].astype(bf16)
            for half in range(halves):
                one = field[at(0, tile, HALO + half * 8), :]
                two = field[at(1, tile, HALO + half * 8), :]
                if side == 0:
                    packed = jnp.where(low, roll(one, NZ), two)
                else:
                    packed = jnp.where(low, one, roll(two, NZ))
                pot_sy[step, side, half] = packed.astype(bf16)
        return exchange(
            2 * step,
            pot_sx.at[step],
            pot_sy.at[step],
            lambda i, j: pot_sy.at[step, j, halves - 1 if i == 0 else 0],
            pot_rx.at[step],
            pot_ry.at[step],
            pot_rc.at[step],
        )

    def common_velocity(t, carry):
        for half in range(halves):
            momenta = []
            for component in range(2):
                gap = [None] * 19
                for direction in range(1, 19, 2):
                    gap[direction] = pop_at(component, direction, t, half) - pop_at(
                        component, direction + 1, t, half
                    )
                momenta.append(
                    (
                        (gap[1] + gap[7]) + (gap[9] + gap[11]) + gap[13],
                        (gap[3] + gap[7]) + (gap[15] - gap[9]) + gap[17],
                        (gap[5] + gap[11]) + (gap[15] - gap[13]) - gap[17],
                    )
                )
            place = spot(t, half)
            inverse = 1.0 / (
                aux[0, place, :] * (1.0 / RELAX_TIMES[0]) + aux[1, place, :] * (1.0 / RELAX_TIMES[1])
            )
            for axis_pos in range(3):
                aux[2 + axis_pos, place, :] = (
                    momenta[0][axis_pos] * (1.0 / RELAX_TIMES[0])
                    + momenta[1][axis_pos] * (1.0 / RELAX_TIMES[1])
                ) * inverse
        return carry

    def receive_potential(step, copies):
        for copy in copies:
            copy.wait()
        for side in range(2):
            row = HALO - 1 if side == 0 else HALO + size_x
            tile = 0 if side == 0 else tiles + 1
            for index in range(2):
                field[across(index, row), :] = pot_rx[step, side, index].astype(f32)

            def unpack(value, start):
                turned = roll(value, NZ)
                one, two = (turned, value) if side == 0 else (value, turned)
                field[at(0, tile, start), :] = one
                field[at(1, tile, start), :] = two

            for half in range(halves):
                unpack(pot_ry[step, side, half].astype(f32), HALO + half * 8)
            for place, (i, j) in enumerate(EDGES):
                if j == side:
                    start = 0 if i == 0 else HALO + size_x
                    unpack(pot_rc[step, place].astype(f32), start)

    def spread_x(tile, carry):
        for half in range(halves):
            start = HALO + half * 8
            place = pl.ds(pl.multiple_of(tile * size_x + half * 8, 8), 8)
            for index in range(2):
                centre = field[at(index, tile, start), :]
                above = field[off(index, tile, start + 1), :]
                below = field[off(index, tile, start - 1), :]
                gap = above - below
                total = 2.0 * centre + (above + below)
                spread[5 * index, place, :] = gap
                spread[5 * index + 1, place, :] = total
                spread[5 * index + 2, place, :] = roll(gap, NZ)
                spread[5 * index + 3, place, :] = roll(total, NZ)
                spread[5 * index + 4, place, :] = roll(centre, NZ)
        return carry

    def pull_of(index, t, half):
        def held(kind, tile):
            place = pl.ds(pl.multiple_of(tile * size_x + half * 8, 8), 8)
            return spread[5 * index + kind, place, :]

        def upper(here, above):
            return jnp.where(low, here, above)

        def lower(here, below):
            return jnp.where(low, below, here)

        gap = held(0, t + 1)
        turned_gap = held(2, t + 1)
        pull_x = 2.0 * gap + (
            upper(turned_gap, held(2, t + 2)) + lower(turned_gap, held(2, t))
        )
        pull_x = pull_x + (z_from_below(gap, turned_gap) + z_from_above(gap, turned_gap))
        turned_total = held(3, t + 1)
        pull_y = upper(turned_total, held(3, t + 2)) - lower(turned_total, held(3, t))
        turned = held(4, t + 1)
        centre = field[at(index, t + 1, HALO + half * 8), :]
        y_above = upper(turned, held(4, t + 2))
        y_below = lower(turned, held(4, t))
        next_tile = field[at(index, t + 2, HALO + half * 8), :]
        previous_tile = field[at(index, t, HALO + half * 8), :]
        turned_y_above = jnp.where(low, next_tile, centre)
        turned_y_below = jnp.where(low, centre, previous_tile)
        gap_y = y_above - y_below
        turned_gap_y = turned_y_above - turned_y_below
        pull_y = pull_y + (z_from_below(gap_y, turned_gap_y) + z_from_above(gap_y, turned_gap_y))
        plane = held(1, t + 1) + (y_above + y_below)
        turned_plane = turned_total + (turned_y_above + turned_y_below)
        pull_z = z_from_above(plane, turned_plane) - z_from_below(plane, turned_plane)
        return pull_x, pull_y, pull_z

    def store_moved(component, direction, t, half, value):
        _, along, upward = velocities[direction]
        if along != 0 or upward != 0:
            turned = roll(value, NZ)
            if along != 0:
                value, turned = turned, value
            if upward == 1:
                value = z_from_below(value, turned)
            elif upward == -1:
                value = z_from_above(value, turned)
        stream[at(19 * component + direction, t + 1, HALO + half * 8), :] = value

    def collide(t, carry):
        for half in range(halves):
            place = spot(t, half)
            fluid = fluid_at(t, half) == 0
            centre = [field[at(index, t + 1, HALO + half * 8), :] for index in range(2)]
            for component in range(2):
                pull = pull_of(component, t, half)
                density = aux[component, place, :]
                scale = (-3.0 * RELAX_TIMES[component] / (36.0 * COUPLING)) * centre[1 - component]
                scale = scale / density
                speed = [
                    3.0 * aux[2 + axis_pos, place, :] + scale * pull[axis_pos] for axis_pos in range(3)
                ]
                square = speed[0] * speed[0] + speed[1] * speed[1] + speed[2] * speed[2]
                level = 1.0 - square * (1.0 / 6.0)
                rate = 1.0 / RELAX_TIMES[component]
                kept = 1.0 - rate
                light = density * (rate / 36.0)
                heavy = density * (rate / 18.0)
                light_level = light * level
                heavy_level = heavy * level

                def settle(direction, equilibrium, own, bounced):
                    relaxed = equilibrium if kept == 0.0 else equilibrium + kept * own
                    store_moved(
                        component, direction, t, half, jnp.where(fluid, relaxed, bounced)
                    )

                rest = pop_at(component, 0, t, half)
                settle(0, 6.0 * heavy_level, rest, rest)
                for direction in range(1, 19, 2):
                    along = None
                    for axis_pos in range(3):
                        part = velocities[direction][axis_pos]
                        if part == 1:
                            along = speed[axis_pos] if along is None else along + speed[axis_pos]
                        elif part == -1:
                            along = along - speed[axis_pos]
                    weighted = (heavy if direction < 7 else light) * along
                    even = (heavy_level if direction < 7 else light_level) + 0.5 * (weighted * along)
                    one = pop_at(component, direction, t, half)
                    two = pop_at(component, direction + 1, t, half)
                    settle(direction, even + weighted, one, two)
                    settle(direction + 1, even - weighted, two, one)
        return carry

    def send_populations(step):
        for side in range(2):
            row = HALO + size_x - 1 if side == 0 else HALO
            tile = tiles if side == 0 else 1
            for component in range(2):
                for place, direction in enumerate(along_x[side]):
                    pop_sx[step, side, 5 * component + place] = stream[
                        across(19 * component + direction, row), :
                    ].astype(bf16)
            for place, direction in enumerate(along_y[side]):
                for half in range(halves):
                    one = stream[at(direction, tile, HALO + half * 8), :]
                    two = stream[at(19 + direction, tile, HALO + half * 8), :]
                    if side == 0:
                        packed = jnp.where(low, one, roll(two, NZ))
                    else:
                        packed = jnp.where(low, roll(one, NZ), two)
                    pop_sy[step, side, place, half] = packed.astype(bf16)
        return exchange(
            2 * step + 1,
            pop_sx.at[step],
            pop_sy.at[step],
            lambda i, j: pop_sy.at[
                step, j, along_y[j].index(along_edge[i, j]), halves - 1 if i == 0 else 0
            ],
            pop_rx.at[step],
            pop_ry.at[step],
            pop_rc.at[step],
        )

    def receive_populations(step, copies):
        for copy in copies:
            copy.wait()
        for side in range(2):
            row = HALO - 1 if side == 0 else HALO + size_x
            tile = 0 if side == 0 else tiles + 1
            for component in range(2):
                for place, direction in enumerate(along_x[side]):
                    stream[across(19 * component + direction, row), :] = pop_rx[
                        step, side, 5 * component + place
                    ].astype(f32)

            def unpack(direction, value, start):
                turned = roll(value, NZ)
                one, two = (value, turned) if side == 0 else (turned, value)
                stream[at(direction, tile, start), :] = one
                stream[at(19 + direction, tile, start), :] = two

            for place, direction in enumerate(along_y[side]):
                for half in range(halves):
                    unpack(
                        direction, pop_ry[step, side, place, half].astype(f32), HALO + half * 8
                    )
            for place, (i, j) in enumerate(EDGES):
                if j == side:
                    start = 0 if i == 0 else HALO + size_x
                    unpack(along_edge[i, j], pop_rc[step, place].astype(f32), start)

    def settle_step(last):
        target = out_ref if last else pops

        def read(t, carry):
            lanes = pl.ds(pl.multiple_of(t * 128, 128), 128)
            for half in range(halves):
                fluid = fluid_at(t, half) == 0
                xglobal = gx * size_x + half * 8 + row_index
                inlet = jnp.logical_and(xglobal == planes_ref[0], fluid)
                outlet = jnp.logical_and(xglobal == planes_ref[1], fluid)
                fixed = jnp.logical_or(inlet, outlet)
                densities = []
                for component in range(2):
                    forced = {}
                    for weight in sorted(set(lattice_weights)):
                        values = [
                            float(np.asarray(weight * level[component], jnp.bfloat16))
                            for level in (INLET_DENSITY, OUTLET_DENSITY)
                        ]
                        forced[weight] = jnp.where(inlet, values[0], values[1])
                    total = None
                    for direction in range(19):
                        step_x, step_y, _ = velocities[direction]
                        index = 19 * component + direction
                        start = HALO + half * 8 - step_x
                        value = stream[off(index, t + 1, start), :]
                        if step_y == 1:
                            value = jnp.where(low, stream[off(index, t, start), :], value)
                        elif step_y == -1:
                            value = jnp.where(low, value, stream[off(index, t + 2, start), :])
                        value = jnp.where(fixed, forced[lattice_weights[direction]], value)
                        narrow = value.astype(bf16)
                        target[component, direction, half * 8 : half * 8 + 8, lanes] = narrow
                        if not last:
                            wide = narrow.astype(f32)
                            total = wide if total is None else total + wide
                    densities.append(total)
                if not last:
                    store_potential(t, half, densities)
            return carry

        lax.fori_loop(0, tiles, read, 0)

    lax.fori_loop(0, tiles, first_density, 0)
    pl.semaphore_wait(barrier, len(targets))
    for step in range(STEPS):
        copies = send_potential(step)
        lax.fori_loop(0, tiles, common_velocity, 0)
        receive_potential(step, copies)
        lax.fori_loop(0, tiles + 2, spread_x, 0)
        lax.fori_loop(0, tiles, collide, 0)
        copies = send_populations(step)
        receive_populations(step, copies)
        settle_step(step == STEPS - 1)


def on_device(nx_devices, ny_devices, populations, wall_class, planes):
    size_x, width = populations.shape[2:]
    tiles = width // 128
    halves = size_x // 8
    rows = size_x + 2 * HALO
    block = (tiles + 2) * rows
    bf16 = jnp.bfloat16
    f32 = jnp.float32
    return pl.pallas_call(
        functools.partial(kernel, nx_devices, ny_devices),
        out_shape=jax.ShapeDtypeStruct(populations.shape, bf16),
        in_specs=[
            pl.BlockSpec(memory_space=pl.ANY),
            pl.BlockSpec(memory_space=pltpu.VMEM),
            pl.BlockSpec(memory_space=pltpu.SMEM),
        ],
        out_specs=pl.BlockSpec(memory_space=pltpu.VMEM),
        scratch_shapes=[
            pltpu.VMEM(populations.shape, bf16),
            pltpu.VMEM((2 * block, 128), f32),
            pltpu.VMEM((10, (tiles + 2) * size_x, 128), f32),
            pltpu.VMEM((5, tiles * size_x, 128), f32),
            pltpu.VMEM((38 * block, 128), f32),
            pltpu.VMEM((STEPS, 2, 2, tiles, 128), bf16),
            pltpu.VMEM((STEPS, 2, halves, 8, 128), bf16),
            pltpu.VMEM((STEPS, 2, 2, tiles, 128), bf16),
            pltpu.VMEM((STEPS, 2, halves, 8, 128), bf16),
            pltpu.VMEM((STEPS, 4, 8, 128), bf16),
            pltpu.VMEM((STEPS, 2, 10, tiles, 128), bf16),
            pltpu.VMEM((STEPS, 2, 5, halves, 8, 128), bf16),
            pltpu.VMEM((STEPS, 2, 10, tiles, 128), bf16),
            pltpu.VMEM((STEPS, 2, 5, halves, 8, 128), bf16),
            pltpu.VMEM((STEPS, 4, 8, 128), bf16),
            pltpu.SemaphoreType.DMA((tiles,)),
            pltpu.SemaphoreType.DMA((2 * STEPS, 8)),
            pltpu.SemaphoreType.DMA((2 * STEPS, 8)),
        ],
        compiler_params=pltpu.CompilerParams(
            collective_id=0, has_side_effects=True, vmem_limit_bytes=40 * 1024 * 1024
        ),
    )(populations, wall_class, planes)


def solution(mesh):
    in_specs = (P(None, None, "gx", "gy"), P("gx", "gy"), P())
    out_specs = P(None, None, "gx", "gy")
    return jax.shard_map(
        functools.partial(on_device, mesh.shape["gx"], mesh.shape["gy"]),
        mesh=mesh,
        in_specs=in_specs,
        out_specs=out_specs,
        check_vma=False,
    )
```

time: 217 us -> 60.8 us (0.28)
  starting transfers between devices: 97.3 us -> 0 us
  Pallas kernels: 0 us -> 56.8 us
  local copies, waits for them, and re-layouts: 46.6 us -> 3.82 us
  waiting for transfers between devices: 40.4 us -> 0 us
  other arithmetic: 28.7 us -> 0 us
  between operations: 2.69 us -> 0.01 us
    ppermute x20 -> x0, starting transfers between devices: 97.3 us -> none  [the longest x8 36.7 us: passed_along(): lax.ppermute(array, axis, [(i, (i + by) % size) for i in range(size)])]
    pallas_call x0 -> x1, Pallas kernels: none -> 56.8 us  [on_device(): pl.pallas_call(functools.partial(kernel, nx_devices, ny_devices), out_sha...]
    ppermute x20 -> x0, waiting for transfers between devices: 40.4 us -> none  [the longest x8 30.7 us: passed_along(): lax.ppermute(array, axis, [(i, (i + by) % size) for i in range(size)])]
    concatenate x164 -> x0, local copies, waits for them, and re-layouts: 28.1 us -> none  [the longest x2 17.9 us: outgoing_faces(): jnp.concatenate([place_rim(from_left, upward_y, blank_y), grown, place_ri...]
    unnamed x186 -> x0, other arithmetic: 15.3 us -> none
    slice x33 -> x0, local copies, waits for them, and re-layouts: 8.4 us -> none  [the longest x5 5.13 us: pick(): lax.slice_in_dim(field, offset + vector[0], offset + vector[0] + size_x,...]
    concatenate x4 -> x0, other arithmetic: 6.81 us -> none  [the longest x2 6.72 us: outgoing_faces(): jnp.concatenate([place_rim(from_below, upward_x, blank_x), collided, plac...]
    add x10 -> x0, other arithmetic: 4.53 us -> none  [the longest x4 2.47 us: densities_of(): total = total + pops[component, direction].astype(jnp.float32)]
  transfers between devices with their start and end apart: 20 -> 0, of which waited for: 6 -> 0; matrix products, arithmetic and copies ran while one was open for 4% -> 0% of each run, Pallas kernels for 0% -> 0%
where the time goes in v1:
time: 60.8 us; the launch traced here: 60.6 us
  Pallas kernels  56.8 us (93%)
  local copies, waits for them, and re-layouts  3.82 us (6%)
    pallas_call x1, Pallas kernels, on_device(): pl.pallas_call(functools.partial(kernel, nx_devices, ny_devices), out_sha...  56.8 us
    unnamed x7, local copies, waits for them, and re-layouts  3.82 us

profile of v1, /device:TPU:7, one launch (start us, length us, event | category | flops | bytes accessed | tf_op | source)
XLA Modules:
  0.0 60.6 jit_solution(15184739592295557789)
XLA Ops:
  0.0 0.0 copy-start
  0.0 1.3 %copy-done = bf16[2,19,16,1024]{3,2,1,0:T(8,128)(2,1)S(1)} copy-done((bf16[2,19,16,1024]{3,2,1,0:T(8,128)(2,1)S(1)}, bf16[2,19,16,1024]{3,2,1,0:T(8,128)(2,1)}, u32[]{:S(2)}) %copy-start) | copy-done | bytes 1245208
  1.3 0.0 copy-start.1
  1.3 0.8 %copy-done.1 = s32[16,1024]{1,0:T(8,128)S(1)} copy-done((s32[16,1024]{1,0:T(8,128)S(1)}, s32[16,1024]{1,0:T(8,128)}, u32[]{:S(2)}) %copy-start.1) | copy-done | bytes 65560
  2.1 0.0 copy-start.2
  2.1 0.7 %copy-done.2 = s32[2]{0:T(128)S(1)} copy-done((s32[2]{0:T(128)S(1)}, s32[2]{0:T(128)}, u32[]{:S(2)}) %copy-start.2) | copy-done | bytes 32
  2.8 56.8 %shard_map.37 = bf16[2,19,16,1024]{3,2,1,0:T(8,128)(2,1)S(1)} custom-call(bf16[2,19,16,1024]{3,2,1,0:T(8,128)(2,1)S(1)} %copy-done, s32[16,1024]{1,0:T(8,128)S(1)} %copy-done.1, s32[2]{0:T(128)S(1)} %copy-done.2), custom_call_target="tpu_custom_call" | custom-call | tf_op jit(solution)/shard_map/pallas_call | solution.py:495
  59.5 1.0 %copy.5 = bf16[2,19,16,1024]{3,2,1,0:T(8,128)(2,1)} copy(bf16[2,19,16,1024]{3,2,1,0:T(8,128)(2,1)S(1)} %shard_map.37) | data formatting | bytes 2490368
Async XLA Ops:
  0.0 1.3 %copy-start = (bf16[2,19,16,1024]{3,2,1,0:T(8,128)(2,1)S(1)}, bf16[2,19,16,1024]{3,2,1,0:T(8,128)(2,1)}, u32[]{:S(2)}) copy-start(bf16[2,19,16,1024]{3,2,1,0:T(8,128)(2,1)} %pops_hbm.1) | copy-start | bytes 3735556
  1.3 0.8 %copy-start.1 = (s32[16,1024]{1,0:T(8,128)S(1)}, s32[16,1024]{1,0:T(8,128)}, u32[]{:S(2)}) copy-start(s32[16,1024]{1,0:T(8,128)} %wall_ref.1) | copy-start | bytes 196612
  2.1 0.7 %copy-start.2 = (s32[2]{0:T(128)S(1)}, s32[2]{0:T(128)}, u32[]{:S(2)}) copy-start(s32[2]{0:T(128)} %planes_ref.1) | copy-start | bytes 28

commit v2 on v1

v2 whole, which is shorter than its diff:
```python
import functools

import jax
import jax.numpy as jnp
import numpy as np
from jax import lax
from jax.experimental import pallas as pl
from jax.experimental.pallas import tpu as pltpu
from jax.sharding import PartitionSpec as P

NZ = 64
STEPS = 2
MESH = pl.DeviceIdType.MESH
velocities = (
    (0, 0, 0),
    (1, 0, 0),
    (-1, 0, 0),
    (0, 1, 0),
    (0, -1, 0),
    (0, 0, 1),
    (0, 0, -1),
    (1, 1, 0),
    (-1, -1, 0),
    (1, -1, 0),
    (-1, 1, 0),
    (1, 0, 1),
    (-1, 0, -1),
    (1, 0, -1),
    (-1, 0, 1),
    (0, 1, 1),
    (0, -1, -1),
    (0, 1, -1),
    (0, -1, 1),
)
lattice_weights = (1.0 / 3.0,) + (1.0 / 18.0,) * 6 + (1.0 / 36.0,) * 12
COUPLING = 2.5
RELAX_TIMES = (1.0, 0.8)
STRENGTHS = (0.0, 0.15, 0.35, 0.6)
INLET_DENSITY = (1.0, 0.03)
OUTLET_DENSITY = (0.03, 1.0)
along_x = ((1, 7, 9, 11, 13), (2, 8, 10, 12, 14))
along_y = ((3, 7, 10, 15, 17), (4, 8, 9, 16, 18))
along_edge = {(0, 0): 7, (1, 1): 8, (0, 1): 9, (1, 0): 10}
EDGES = ((0, 0), (0, 1), (1, 0), (1, 1))

HALO = 8


def opposite(direction):
    if direction == 0:
        return 0
    return direction + 1 if direction % 2 == 1 else direction - 1


def face_order(side, half, halves):
    edge = along_edge[0 if half == halves - 1 else 1, side]
    return (edge,) + tuple(d for d in along_y[side] if d != edge)


X_PARTS = 4 + 5 + 10
Y_PARTS = 2 + 3 + 5
EDGE_PARTS = 2 + 3 + 1


def kernel(
    nx_devices,
    ny_devices,
    pops_hbm,
    wall_hbm,
    planes_hbm,
    out_ref,
    pops,
    wall_ref,
    planes_ref,
    field,
    spread,
    aux,
    held_x,
    held_y,
    stream,
    send_x,
    send_y,
    recv_x,
    recv_y,
    recv_c,
    in_sem,
    send_sem,
    recv_sem,
):
    size_x = pops.shape[2]
    tiles = pops.shape[3] // 128
    halves = size_x // 8
    rows = size_x + 2 * HALO
    block = (tiles + 2) * rows
    first_row = HALO
    last_row = HALO + size_x - 1
    f32 = jnp.float32
    bf16 = jnp.bfloat16

    gx = lax.axis_index("gx")
    gy = lax.axis_index("gy")
    near_x = (lax.rem(gx + 1, nx_devices), lax.rem(gx + nx_devices - 1, nx_devices))
    near_y = (lax.rem(gy + 1, ny_devices), lax.rem(gy + ny_devices - 1, ny_devices))

    barrier = pltpu.get_barrier_semaphore()
    targets = [(near_x[0], gy), (near_x[1], gy), (gx, near_y[0]), (gx, near_y[1])]
    targets += [(near_x[i], near_y[j]) for i, j in EDGES]
    for target in targets:
        pl.semaphore_signal(barrier, inc=1, device_id=target, device_id_type=MESH)

    def load_in(t):
        lanes = pl.ds(pl.multiple_of(t * 128, 128), 128)
        return pltpu.make_async_copy(
            pops_hbm.at[:, :, :, lanes], pops.at[:, :, :, lanes], in_sem.at[t]
        )

    load_wall = pltpu.make_async_copy(wall_hbm, wall_ref, in_sem.at[tiles])
    load_planes = pltpu.make_async_copy(planes_hbm, planes_ref, in_sem.at[tiles + 1])
    load_wall.start()
    for t in range(tiles):
        load_in(t).start()
    load_planes.start()

    lane = lax.broadcasted_iota(jnp.int32, (8, 128), 1)
    row_index = lax.broadcasted_iota(jnp.int32, (8, 128), 0)
    low = lane < NZ
    first_z = jnp.logical_or(lane == 0, lane == NZ)
    last_z = jnp.logical_or(lane == NZ - 1, lane == 2 * NZ - 1)

    def roll(value, by):
        return pltpu.roll(value, by % 128, 1)

    def z_from_below(value, turned):
        return roll(jnp.where(last_z, turned, value), 1)

    def z_from_above(value, turned):
        return roll(jnp.where(first_z, turned, value), -1)

    def at(index, tile, row):
        return pl.ds(pl.multiple_of(index * block + tile * rows + row, 8), 8)

    def off(index, tile, row):
        return pl.ds(index * block + tile * rows + row, 8)

    def across(index, row, by=0):
        return pl.ds(index * block + (1 + by) * rows + row, tiles, stride=rows)

    def wall_at(t, half):
        lanes = pl.ds(pl.multiple_of(t * 128, 128), 128)
        return wall_ref[half * 8 : half * 8 + 8, lanes]

    def pop_at(component, direction, t, half):
        lanes = pl.ds(pl.multiple_of(t * 128, 128), 128)
        return pops[component, direction, half * 8 : half * 8 + 8, lanes].astype(f32)

    rates = [1.0 / value for value in RELAX_TIMES]
    gains = [-3.0 * value / (36.0 * COUPLING) for value in RELAX_TIMES]

    def store_potential(t, half, densities):
        wall = wall_at(t, half)
        fluid = wall == 0
        strength = jnp.where(
            wall == 1, STRENGTHS[1], jnp.where(wall == 2, STRENGTHS[2], STRENGTHS[3])
        )
        oil = COUPLING * (1.0 - jnp.exp(-densities[0]))
        brine = COUPLING * (1.0 - jnp.exp(-densities[1]))
        field[at(0, t + 1, HALO + half * 8), :] = jnp.where(fluid, brine, strength)
        field[at(1, t + 1, HALO + half * 8), :] = jnp.where(fluid, oil, -strength)
        aux[at(0, t + 1, HALO + half * 8), :] = densities[0]
        aux[at(1, t + 1, HALO + half * 8), :] = densities[1]

    def first_density(t, carry):
        load_in(t).wait()
        for half in range(halves):
            densities = []
            for component in range(2):
                total = pop_at(component, 0, t, half)
                for direction in range(1, 19):
                    total = total + pop_at(component, direction, t, half)
                densities.append(total)
            store_potential(t, half, densities)
        return carry

    def kept_part(component, fluid, own, bounced):
        kept = 1.0 - rates[component]
        return jnp.where(fluid, kept * own if kept != 0.0 else 0.0, bounced)

    def moments(t, carry):
        for half in range(halves):
            place = t + 1, HALO + half * 8
            fluid = wall_at(t, half) == 0
            side = 0 if half == halves - 1 else 1
            momenta = []
            for component in range(2):
                gap = [None] * 19
                for direction in range(1, 19, 2):
                    one = pop_at(component, direction, t, half)
                    two = pop_at(component, direction + 1, t, half)
                    gap[direction] = one - two
                    for toward, own, bounced in ((direction, one, two), (direction + 1, two, one)):
                        if toward in along_x[side]:
                            index = 5 * component + along_x[side].index(toward)
                            start = pl.multiple_of((index * tiles + t) * size_x + half * 8, 8)
                            held_x[pl.ds(start, 8), :] = kept_part(component, fluid, own, bounced)
                momenta.append(
                    (
                        (gap[1] + gap[7]) + (gap[9] + gap[11]) + gap[13],
                        (gap[3] + gap[7]) + (gap[15] - gap[9]) + gap[17],
                        (gap[5] + gap[11]) + (gap[15] - gap[13]) - gap[17],
                    )
                )
            densities = [aux[at(component, *place), :] for component in range(2)]
            inverse = 3.0 / (densities[0] * rates[0] + densities[1] * rates[1])
            for axis_pos in range(3):
                aux[at(2 + axis_pos, *place), :] = (
                    momenta[0][axis_pos] * rates[0] + momenta[1][axis_pos] * rates[1]
                ) * inverse
            for component in range(2):
                gain = gains[component] * field[at(1 - component, *place), :] / densities[component]
                aux[at(5 + component, *place), :] = jnp.where(fluid, gain, 0.0)
                aux[at(component, *place), :] = jnp.where(fluid, densities[component], 0.0)
        return carry

    def pack(side, one, two):
        turned = roll(two, NZ)
        return jnp.where(low, turned, one) if side == 0 else jnp.where(low, one, turned)

    def send_edges(step):
        for side in range(2):
            row, inner = (last_row, last_row - 1) if side == 0 else (first_row, first_row + 1)
            for index in range(2):
                send_x[step, side, index] = field[across(index, row), :].astype(bf16)
                send_x[step, side, 2 + index] = field[across(index, inner), :].astype(bf16)
            for index in range(5):
                send_x[step, side, 4 + index] = aux[across(index, row), :].astype(bf16)
            for index in range(10):
                start = index * tiles * size_x + row - HALO
                part = held_x[pl.ds(start, tiles, stride=size_x), :]
                send_x[step, side, 9 + index] = part.astype(bf16)
            t = tiles - 1 if side == 0 else 0
            for half in range(halves):
                place = t + 1, HALO + half * 8
                fluid = wall_at(t, half) == 0
                for index in range(2):
                    send_y[step, side, half, index] = field[at(index, *place), :].astype(bf16)
                for index, (one, two) in enumerate(((0, 1), (2, 3), (4, 4))):
                    packed = pack(side, aux[at(one, *place), :], aux[at(two, *place), :])
                    send_y[step, side, half, 2 + index] = packed.astype(bf16)
                for index, direction in enumerate(face_order(side, half, halves)):
                    parts = [
                        kept_part(
                            component,
                            fluid,
                            pop_at(component, direction, t, half),
                            pop_at(component, opposite(direction), t, half),
                        )
                        for component in range(2)
                    ]
                    send_y[step, side, half, 5 + index] = pack(side, *parts).astype(bf16)
        copies = []
        for place, (i, j) in enumerate(EDGES):
            source = send_y.at[step, j, halves - 1 if i == 0 else 0, pl.ds(0, EDGE_PARTS)]
            copies.append((source, recv_c.at[step, place], (near_x[i], near_y[j])))
        for side in range(2):
            copies.append((send_x.at[step, side], recv_x.at[step, side], (near_x[side], gy)))
            copies.append((send_y.at[step, side], recv_y.at[step, side], (gx, near_y[side])))
        started = []
        for place, (source, target, device) in enumerate(copies):
            copy = pltpu.make_async_remote_copy(
                src_ref=source,
                dst_ref=target,
                send_sem=send_sem.at[step, place],
                recv_sem=recv_sem.at[step, place],
                device_id=device,
                device_id_type=MESH,
            )
            copy.start()
            started.append(copy)
        return started

    def gain_of(component, source, density):
        return jnp.where(density == 0.0, 0.0, gains[component] * source / density)

    def receive_edges(step, copies):
        for copy in copies:
            copy.wait()
        for side in range(2):
            row, outer = (first_row - 1, first_row - 2) if side == 0 else (last_row + 1, last_row + 2)
            sources = []
            for index in range(2):
                source = recv_x[step, side, index].astype(f32)
                sources.append(source)
                field[across(index, row), :] = source
                field[across(index, outer), :] = recv_x[step, side, 2 + index].astype(f32)
            for index in range(5):
                value = recv_x[step, side, 4 + index].astype(f32)
                aux[across(index, row), :] = value
                if index < 2:
                    aux[across(5 + index, row), :] = gain_of(index, sources[1 - index], value)
            tile = 0 if side == 0 else tiles + 1

            def unpack(load, start, order):
                sources = [load(index) for index in range(2)]
                for index in range(2):
                    field[at(index, tile, start), :] = sources[index]
                for index, (one, two) in enumerate(((0, 1), (2, 3), (4, None))):
                    value = load(2 + index)
                    turned = roll(value, NZ)
                    aux[at(one, tile, start), :] = value
                    if two is not None:
                        aux[at(two, tile, start), :] = turned
                    if index == 0:
                        for component, density in ((0, value), (1, turned)):
                            gain = gain_of(component, sources[1 - component], density)
                            aux[at(5 + component, tile, start), :] = gain
                for index, direction in enumerate(order):
                    value = load(5 + index)
                    turned = roll(value, NZ)
                    place = along_y[side].index(direction)
                    for component, part in ((0, value), (1, turned)):
                        base = ((5 * component + place) * 2 + side) * rows
                        held_y[pl.ds(base + start, 8), :] = part

            for half in range(halves):
                unpack(
                    lambda index: recv_y[step, side, half, index].astype(f32),
                    HALO + half * 8,
                    face_order(side, half, halves),
                )
            for place, (i, j) in enumerate(EDGES):
                if j == side:
                    unpack(
                        lambda index: recv_c[step, place, index].astype(f32),
                        0 if i == 0 else HALO + size_x,
                        (along_edge[i, j],),
                    )

    windows = tuple(range(first_row - 1, last_row - 6, 8)) + (last_row - 6,)

    def spread_x(tile, carry):
        for start in windows:
            for index in range(2):
                centre = field[off(index, tile, start), :]
                above = field[off(index, tile, start + 1), :]
                below = field[off(index, tile, start - 1), :]
                gap = above - below
                total = 2.0 * centre + (above + below)
                spread[off(5 * index, tile, start), :] = gap
                spread[off(5 * index + 1, tile, start), :] = total
                spread[off(5 * index + 2, tile, start), :] = roll(gap, NZ)
                spread[off(5 * index + 3, tile, start), :] = roll(total, NZ)
                spread[off(5 * index + 4, tile, start), :] = roll(centre, NZ)
        return carry

    def pull_of(index, where):
        def held(kind, by=0):
            return spread[where(5 * index + kind, by), :]

        def upper(here, above):
            return jnp.where(low, here, above)

        def lower(here, below):
            return jnp.where(low, below, here)

        gap = held(0)
        turned_gap = held(2)
        pull_x = 2.0 * gap + (upper(turned_gap, held(2, 1)) + lower(turned_gap, held(2, -1)))
        pull_x = pull_x + (z_from_below(gap, turned_gap) + z_from_above(gap, turned_gap))
        turned_total = held(3)
        pull_y = upper(turned_total, held(3, 1)) - lower(turned_total, held(3, -1))
        turned = held(4)
        y_above = upper(turned, held(4, 1))
        y_below = lower(turned, held(4, -1))
        centre = field[where(index, 0), :]
        turned_y_above = jnp.where(low, field[where(index, 1), :], centre)
        turned_y_below = jnp.where(low, centre, field[where(index, -1), :])
        gap_y = y_above - y_below
        turned_gap_y = turned_y_above - turned_y_below
        pull_y = pull_y + (z_from_below(gap_y, turned_gap_y) + z_from_above(gap_y, turned_gap_y))
        plane = held(1) + (y_above + y_below)
        turned_plane = turned_total + (turned_y_above + turned_y_below)
        pull_z = z_from_above(plane, turned_plane) - z_from_below(plane, turned_plane)
        return pull_x, pull_y, pull_z

    def moved(direction, value):
        _, along, upward = velocities[direction]
        if along != 0 or upward != 0:
            turned = roll(value, NZ)
            if along != 0:
                value, turned = turned, value
            if upward == 1:
                value = z_from_below(value, turned)
            elif upward == -1:
                value = z_from_above(value, turned)
        return value

    def equilibria(component, where, directions):
        pull = pull_of(component, where)
        density = aux[where(component, 0), :]
        gain = aux[where(5 + component, 0), :]
        speed = [aux[where(2 + axis_pos, 0), :] + gain * pull[axis_pos] for axis_pos in range(3)]
        square = speed[0] * speed[0] + speed[1] * speed[1] + speed[2] * speed[2]
        level = 1.0 - square * (1.0 / 6.0)
        light = density * (rates[component] / 36.0)
        heavy = density * (rates[component] / 18.0)
        light_level = light * level
        heavy_level = heavy * level
        if 0 in directions:
            yield 0, 6.0 * heavy_level
        for direction in range(1, 19, 2):
            if direction not in directions and direction + 1 not in directions:
                continue
            along = None
            for axis_pos in range(3):
                part = velocities[direction][axis_pos]
                if part == 1:
                    along = speed[axis_pos] if along is None else along + speed[axis_pos]
                elif part == -1:
                    along = along - speed[axis_pos]
            weighted = (heavy if direction < 7 else light) * along
            even = (heavy_level if direction < 7 else light_level) + 0.5 * (weighted * along)
            if direction in directions:
                yield direction, even + weighted
            if direction + 1 in directions:
                yield direction + 1, even - weighted

    def collide(t, carry):
        for half in range(halves):
            fluid = wall_at(t, half) == 0

            def where(index, by):
                return at(index, t + 1 + by, HALO + half * 8)

            for component in range(2):
                kept = 1.0 - rates[component]
                for direction, relaxed in equilibria(component, where, range(19)):
                    if kept != 0.0:
                        relaxed = relaxed + kept * pop_at(component, direction, t, half)
                    bounced = pop_at(component, opposite(direction), t, half)
                    value = moved(direction, jnp.where(fluid, relaxed, bounced))
                    stream[where(19 * component + direction, 0), :] = value
        return carry

    def collide_outside(step):
        for side in range(2):
            row = first_row - 1 if side == 0 else last_row + 1
            for component in range(2):

                def where(index, by):
                    return across(index, row, by)

                for direction, relaxed in equilibria(component, where, along_x[side]):
                    place = 5 * component + along_x[side].index(direction)
                    value = relaxed + recv_x[step, side, 9 + place].astype(f32)
                    stream[where(19 * component + direction, 0), :] = moved(direction, value)
            tile = 0 if side == 0 else tiles + 1
            for start in windows:
                for component in range(2):

                    def where(index, by):
                        return off(index, min(max(tile + by, 0), tiles + 1), start)

                    for direction, relaxed in equilibria(component, where, along_y[side]):
                        place = 5 * component + along_y[side].index(direction)
                        part = held_y[pl.ds((place * 2 + side) * rows + start, 8), :]
                        value = moved(direction, relaxed + part)
                        stream[where(19 * component + direction, 0), :] = value

    def settle_step(last):
        target = out_ref if last else pops

        def read(t, carry):
            lanes = pl.ds(pl.multiple_of(t * 128, 128), 128)
            for half in range(halves):
                fluid = wall_at(t, half) == 0
                xglobal = gx * size_x + half * 8 + row_index
                inlet = jnp.logical_and(xglobal == planes_ref[0], fluid)
                outlet = jnp.logical_and(xglobal == planes_ref[1], fluid)
                fixed = jnp.logical_or(inlet, outlet)
                densities = []
                for component in range(2):
                    forced = {}
                    for weight in sorted(set(lattice_weights)):
                        values = [
                            float(np.asarray(weight * level[component], jnp.bfloat16))
                            for level in (INLET_DENSITY, OUTLET_DENSITY)
                        ]
                        forced[weight] = jnp.where(inlet, values[0], values[1])
                    total = None
                    for direction in range(19):
                        step_x, step_y, _ = velocities[direction]
                        index = 19 * component + direction
                        start = HALO + half * 8 - step_x
                        value = stream[off(index, t + 1, start), :]
                        if step_y == 1:
                            value = jnp.where(low, stream[off(index, t, start), :], value)
                        elif step_y == -1:
                            value = jnp.where(low, value, stream[off(index, t + 2, start), :])
                        value = jnp.where(fixed, forced[lattice_weights[direction]], value)
                        narrow = value.astype(bf16)
                        target[component, direction, half * 8 : half * 8 + 8, lanes] = narrow
                        if not last:
                            wide = narrow.astype(f32)
                            total = wide if total is None else total + wide
                    densities.append(total)
                if not last:
                    store_potential(t, half, densities)
            return carry

        lax.fori_loop(0, tiles, read, 0)

    load_wall.wait()
    lax.fori_loop(0, tiles, first_density, 0)
    load_planes.wait()
    lax.fori_loop(0, tiles, moments, 0)
    pl.semaphore_wait(barrier, len(targets))
    for step in range(STEPS):
        if step > 0:
            lax.fori_loop(0, tiles, moments, 0)
        copies = send_edges(step)
        receive_edges(step, copies)
        lax.fori_loop(0, tiles + 2, spread_x, 0)
        collide_outside(step)
        lax.fori_loop(0, tiles, collide, 0)
        settle_step(step == STEPS - 1)


def on_device(nx_devices, ny_devices, populations, wall_class, planes):
    size_x, width = populations.shape[2:]
    tiles = width // 128
    halves = size_x // 8
    rows = size_x + 2 * HALO
    block = (tiles + 2) * rows
    bf16 = jnp.bfloat16
    f32 = jnp.float32
    return pl.pallas_call(
        functools.partial(kernel, nx_devices, ny_devices),
        out_shape=jax.ShapeDtypeStruct(populations.shape, bf16),
        in_specs=[pl.BlockSpec(memory_space=pltpu.HBM)] * 3,
        out_specs=pl.BlockSpec(memory_space=pltpu.VMEM),
        scratch_shapes=[
            pltpu.VMEM(populations.shape, bf16),
            pltpu.VMEM(wall_class.shape, wall_class.dtype),
            pltpu.SMEM(planes.shape, planes.dtype),
            pltpu.VMEM((2 * block, 128), f32),
            pltpu.VMEM((10 * block, 128), f32),
            pltpu.VMEM((7 * block, 128), f32),
            pltpu.VMEM((10 * tiles * size_x, 128), f32),
            pltpu.VMEM((20 * rows, 128), f32),
            pltpu.VMEM((38 * block, 128), f32),
            pltpu.VMEM((STEPS, 2, X_PARTS, tiles, 128), bf16),
            pltpu.VMEM((STEPS, 2, halves, Y_PARTS, 8, 128), bf16),
            pltpu.VMEM((STEPS, 2, X_PARTS, tiles, 128), bf16),
            pltpu.VMEM((STEPS, 2, halves, Y_PARTS, 8, 128), bf16),
            pltpu.VMEM((STEPS, 4, EDGE_PARTS, 8, 128), bf16),
            pltpu.SemaphoreType.DMA((tiles + 2,)),
            pltpu.SemaphoreType.DMA((STEPS, 8)),
            pltpu.SemaphoreType.DMA((STEPS, 8)),
        ],
        compiler_params=pltpu.CompilerParams(
            collective_id=0, has_side_effects=True, vmem_limit_bytes=40 * 1024 * 1024
        ),
    )(*[pltpu.with_memory_space_constraint(v, pltpu.HBM) for v in (populations, wall_class, planes)])


def solution(mesh):
    in_specs = (P(None, None, "gx", "gy"), P("gx", "gy"), P())
    out_specs = P(None, None, "gx", "gy")
    return jax.shard_map(
        functools.partial(on_device, mesh.shape["gx"], mesh.shape["gy"]),
        mesh=mesh,
        in_specs=in_specs,
        out_specs=out_specs,
        check_vma=False,
    )
```

time: 60.8 us -> 44 us (0.72)
  Pallas kernels: 56.8 us -> 42.8 us
  local copies, waits for them, and re-layouts: 3.82 us -> 1.04 us
    pallas_call x1, Pallas kernels: 56.8 us -> 42.8 us  [on_device(): pl.pallas_call(functools.partial(kernel, nx_devices, ny_devices), out_sha...]
    unnamed x7 -> x1, local copies, waits for them, and re-layouts: 3.82 us -> 1.04 us
where the time goes in v2:
time: 44 us; the launch traced here: 43.9 us
  Pallas kernels  42.8 us (97%)
  local copies, waits for them, and re-layouts  1.04 us (2%)
    pallas_call x1, Pallas kernels, on_device(): pl.pallas_call(functools.partial(kernel, nx_devices, ny_devices), out_sha...  42.8 us
    unnamed x1, local copies, waits for them, and re-layouts  1.04 us

profile of v2, /device:TPU:7, one launch (start us, length us, event | category | flops | bytes accessed | tf_op | source)
XLA Modules:
  0.0 43.9 jit_solution(7078248928524164545)
XLA Ops:
  0.0 42.8 %shard_map.37 = bf16[2,19,16,1024]{3,2,1,0:T(8,128)(2,1)S(1)} custom-call(bf16[2,19,16,1024]{3,2,1,0:T(8,128)(2,1)} %pops_hbm.1, s32[16,1024]{1,0:T(8,128)} %wall_hbm.1, s32[2]{0:T(128)} %planes_hbm.1), custom_call_target="tpu_custom_call" | custom-call | tf_op jit(solution)/shard_map/pallas_call | solution.py:536
  42.8 1.0 %copy.5 = bf16[2,19,16,1024]{3,2,1,0:T(8,128)(2,1)} copy(bf16[2,19,16,1024]{3,2,1,0:T(8,128)(2,1)S(1)} %shard_map.37) | data formatting | bytes 2490368

commit v3 on v2

--- a/solution.py
+++ b/solution.py
@@ -156,69 +156,57 @@
     rates = [1.0 / value for value in RELAX_TIMES]
     gains = [-3.0 * value / (36.0 * COUPLING) for value in RELAX_TIMES]
 
-    def store_potential(t, half, densities):
+    def kept_part(component, fluid, own, bounced):
+        kept = 1.0 - rates[component]
+        return jnp.where(fluid, kept * own if kept != 0.0 else 0.0, bounced)
+
+    def absorb(t, half, get):
+        place = t + 1, HALO + half * 8
         wall = wall_at(t, half)
         fluid = wall == 0
+        side = 0 if half == halves - 1 else 1
+        densities, momenta = [], []
+        for component in range(2):
+            total = get(component, 0)
+            parts = [None] * 3
+            for direction in range(1, 19, 2):
+                one, two = get(component, direction), get(component, direction + 1)
+                total = total + (one + two)
+                gap = one - two
+                for axis_pos in range(3):
+                    along = velocities[direction][axis_pos]
+                    if along != 0:
+                        if parts[axis_pos] is None:
+                            parts[axis_pos] = gap
+                        else:
+                            parts[axis_pos] = parts[axis_pos] + gap if along == 1 else parts[axis_pos] - gap
+                for toward, own, bounced in ((direction, one, two), (direction + 1, two, one)):
+                    if toward in along_x[side]:
+                        index = 5 * component + along_x[side].index(toward)
+                        start = pl.multiple_of((index * tiles + t) * size_x + half * 8, 8)
+                        held_x[pl.ds(start, 8), :] = kept_part(component, fluid, own, bounced)
+            densities.append(total)
+            momenta.append(parts)
         strength = jnp.where(
             wall == 1, STRENGTHS[1], jnp.where(wall == 2, STRENGTHS[2], STRENGTHS[3])
         )
-        oil = COUPLING * (1.0 - jnp.exp(-densities[0]))
-        brine = COUPLING * (1.0 - jnp.exp(-densities[1]))
-        field[at(0, t + 1, HALO + half * 8), :] = jnp.where(fluid, brine, strength)
-        field[at(1, t + 1, HALO + half * 8), :] = jnp.where(fluid, oil, -strength)
-        aux[at(0, t + 1, HALO + half * 8), :] = densities[0]
-        aux[at(1, t + 1, HALO + half * 8), :] = densities[1]
-
-    def first_density(t, carry):
+        pushes = [COUPLING * (1.0 - jnp.exp(-densities[component])) for component in range(2)]
+        field[at(0, *place), :] = jnp.where(fluid, pushes[1], strength)
+        field[at(1, *place), :] = jnp.where(fluid, pushes[0], -strength)
+        inverse = 3.0 / (densities[0] * rates[0] + densities[1] * rates[1])
+        for axis_pos in range(3):
+            aux[at(2 + axis_pos, *place), :] = (
+                momenta[0][axis_pos] * rates[0] + momenta[1][axis_pos] * rates[1]
+            ) * inverse
+        for component in range(2):
+            gain = gains[component] * pushes[component] / densities[component]
+            aux[at(5 + component, *place), :] = jnp.where(fluid, gain, 0.0)
+            aux[at(component, *place), :] = jnp.where(fluid, densities[component], 0.0)
+
+    def first_absorb(t, carry):
         load_in(t).wait()
         for half in range(halves):
-            densities = []
-            for component in range(2):
-                total = pop_at(component, 0, t, half)
-                for direction in range(1, 19):
-                    total = total + pop_at(component, direction, t, half)
-                densities.append(total)
-            store_potential(t, half, densities)
-        return carry
-
-    def kept_part(component, fluid, own, bounced):
-        kept = 1.0 - rates[component]
-        return jnp.where(fluid, kept * own if kept != 0.0 else 0.0, bounced)
-
-    def moments(t, carry):
-        for half in range(halves):
-            place = t + 1, HALO + half * 8
-            fluid = wall_at(t, half) == 0
-            side = 0 if half == halves - 1 else 1
-            momenta = []
-            for component in range(2):
-                gap = [None] * 19
-                for direction in range(1, 19, 2):
-                    one = pop_at(component, direction, t, half)
-                    two = pop_at(component, direction + 1, t, half)
-                    gap[direction] = one - two
-                    for toward, own, bounced in ((direction, one, two), (direction + 1, two, one)):
-                        if toward in along_x[side]:
-                            index = 5 * component + along_x[side].index(toward)
-                            start = pl.multiple_of((index * tiles + t) * size_x + half * 8, 8)
-                            held_x[pl.ds(start, 8), :] = kept_part(component, fluid, own, bounced)
-                momenta.append(
-                    (
-                        (gap[1] + gap[7]) + (gap[9] + gap[11]) + gap[13],
-                        (gap[3] + gap[7]) + (gap[15] - gap[9]) + gap[17],
-                        (gap[5] + gap[11]) + (gap[15] - gap[13]) - gap[17],
-                    )
-                )
-            densities = [aux[at(component, *place), :] for component in range(2)]
-            inverse = 3.0 / (densities[0] * rates[0] + densities[1] * rates[1])
-            for axis_pos in range(3):
-                aux[at(2 + axis_pos, *place), :] = (
-                    momenta[0][axis_pos] * rates[0] + momenta[1][axis_pos] * rates[1]
-                ) * inverse
-            for component in range(2):
-                gain = gains[component] * field[at(1 - component, *place), :] / densities[component]
-                aux[at(5 + component, *place), :] = jnp.where(fluid, gain, 0.0)
-                aux[at(component, *place), :] = jnp.where(fluid, densities[component], 0.0)
+            absorb(t, half, lambda component, direction: pop_at(component, direction, t, half))
         return carry
 
     def pack(side, one, two):
@@ -281,76 +269,90 @@
     def gain_of(component, source, density):
         return jnp.where(density == 0.0, 0.0, gains[component] * source / density)
 
-    def receive_edges(step, copies):
-        for copy in copies:
-            copy.wait()
+    def unpack_x(step, side):
+        row, outer = (first_row - 1, first_row - 2) if side == 0 else (last_row + 1, last_row + 2)
+        sources = []
+        for index in range(2):
+            source = recv_x[step, side, index].astype(f32)
+            sources.append(source)
+            field[across(index, row), :] = source
+            field[across(index, outer), :] = recv_x[step, side, 2 + index].astype(f32)
+        for index in range(5):
+            value = recv_x[step, side, 4 + index].astype(f32)
+            aux[across(index, row), :] = value
+            if index < 2:
+                aux[across(5 + index, row), :] = gain_of(index, sources[1 - index], value)
+
+    def unpack_y(side, load, start, order):
+        tile = 0 if side == 0 else tiles + 1
+        sources = [load(index) for index in range(2)]
+        for index in range(2):
+            field[at(index, tile, start), :] = sources[index]
+        for index, (one, two) in enumerate(((0, 1), (2, 3), (4, None))):
+            value = load(2 + index)
+            turned = roll(value, NZ)
+            aux[at(one, tile, start), :] = value
+            if two is not None:
+                aux[at(two, tile, start), :] = turned
+            if index == 0:
+                for component, density in ((0, value), (1, turned)):
+                    gain = gain_of(component, sources[1 - component], density)
+                    aux[at(5 + component, tile, start), :] = gain
+        for index, direction in enumerate(order):
+            value = load(5 + index)
+            turned = roll(value, NZ)
+            place = along_y[side].index(direction)
+            for component, part in ((0, value), (1, turned)):
+                base = ((5 * component + place) * 2 + side) * rows
+                held_y[pl.ds(base + start, 8), :] = part
+
+    def receive_faces(step, copies):
+        for copy in copies[len(EDGES) :]:
+            copy.wait_recv()
         for side in range(2):
-            row, outer = (first_row - 1, first_row - 2) if side == 0 else (last_row + 1, last_row + 2)
-            sources = []
-            for index in range(2):
-                source = recv_x[step, side, index].astype(f32)
-                sources.append(source)
-                field[across(index, row), :] = source
-                field[across(index, outer), :] = recv_x[step, side, 2 + index].astype(f32)
-            for index in range(5):
-                value = recv_x[step, side, 4 + index].astype(f32)
-                aux[across(index, row), :] = value
-                if index < 2:
-                    aux[across(5 + index, row), :] = gain_of(index, sources[1 - index], value)
-            tile = 0 if side == 0 else tiles + 1
-
-            def unpack(load, start, order):
-                sources = [load(index) for index in range(2)]
-                for index in range(2):
-                    field[at(index, tile, start), :] = sources[index]
-                for index, (one, two) in enumerate(((0, 1), (2, 3), (4, None))):
-                    value = load(2 + index)
-                    turned = roll(value, NZ)
-                    aux[at(one, tile, start), :] = value
-                    if two is not None:
-                        aux[at(two, tile, start), :] = turned
-                    if index == 0:
-                        for component, density in ((0, value), (1, turned)):
-                            gain = gain_of(component, sources[1 - component], density)
-                            aux[at(5 + component, tile, start), :] = gain
-                for index, direction in enumerate(order):
-                    value = load(5 + index)
-                    turned = roll(value, NZ)
-                    place = along_y[side].index(direction)
-                    for component, part in ((0, value), (1, turned)):
-                        base = ((5 * component + place) * 2 + side) * rows
-                        held_y[pl.ds(base + start, 8), :] = part
-
+            unpack_x(step, side)
             for half in range(halves):
-                unpack(
+                unpack_y(
+                    side,
                     lambda index: recv_y[step, side, half, index].astype(f32),
                     HALO + half * 8,
                     face_order(side, half, halves),
                 )
-            for place, (i, j) in enumerate(EDGES):
-                if j == side:
-                    unpack(
-                        lambda index: recv_c[step, place, index].astype(f32),
-                        0 if i == 0 else HALO + size_x,
-                        (along_edge[i, j],),
-                    )
-
-    windows = tuple(range(first_row - 1, last_row - 6, 8)) + (last_row - 6,)
-
-    def spread_x(tile, carry):
-        for start in windows:
-            for index in range(2):
-                centre = field[off(index, tile, start), :]
-                above = field[off(index, tile, start + 1), :]
-                below = field[off(index, tile, start - 1), :]
-                gap = above - below
-                total = 2.0 * centre + (above + below)
-                spread[off(5 * index, tile, start), :] = gap
-                spread[off(5 * index + 1, tile, start), :] = total
-                spread[off(5 * index + 2, tile, start), :] = roll(gap, NZ)
-                spread[off(5 * index + 3, tile, start), :] = roll(total, NZ)
-                spread[off(5 * index + 4, tile, start), :] = roll(centre, NZ)
-        return carry
+
+    def receive_corners(step, copies):
+        for copy in copies[: len(EDGES)]:
+            copy.wait_recv()
+        for place, (i, j) in enumerate(EDGES):
+            unpack_y(
+                j,
+                lambda index: recv_c[step, place, index].astype(f32),
+                0 if i == 0 else HALO + size_x,
+                (along_edge[i, j],),
+            )
+
+    inner_windows = tuple(range(first_row, last_row, 8))
+    outer_windows = (first_row - 1, last_row - 6)
+    middle_windows = tuple(range(first_row + 7, last_row - 6, 8))
+
+    def spread_at(where):
+        for index in range(2):
+            centre = field[where(index, 0), :]
+            above = field[where(index, 1), :]
+            below = field[where(index, -1), :]
+            gap = above - below
+            total = 2.0 * centre + (above + below)
+            spread[where(5 * index, 0), :] = gap
+            spread[where(5 * index + 1, 0), :] = total
+            spread[where(5 * index + 2, 0), :] = roll(gap, NZ)
+            spread[where(5 * index + 3, 0), :] = roll(total, NZ)
+            spread[where(5 * index + 4, 0), :] = roll(centre, NZ)
+
+    def spread_tile(tile, starts):
+        for start in starts:
+            spread_at(lambda index, by: off(index, tile, start + by))
+
+    def spread_row(row):
+        spread_at(lambda index, by: across(index, row + by))
 
     def pull_of(index, where):
         def held(kind, by=0):
@@ -394,9 +396,11 @@
                 value = z_from_above(value, turned)
         return value
 
-    def equilibria(component, where, directions):
+    def equilibria(component, where, directions, left_out=None):
         pull = pull_of(component, where)
         density = aux[where(component, 0), :]
+        if left_out is not None:
+            density = jnp.where(left_out, 0.0, density)
         gain = aux[where(5 + component, 0), :]
         speed = [aux[where(2 + axis_pos, 0), :] + gain * pull[axis_pos] for axis_pos in range(3)]
         square = speed[0] * speed[0] + speed[1] * speed[1] + speed[2] * speed[2]
@@ -424,47 +428,58 @@
             if direction + 1 in directions:
                 yield direction + 1, even - weighted
 
-    def collide(t, carry):
+    def collide(t):
         for half in range(halves):
             fluid = wall_at(t, half) == 0
+            left_out = row_index == (7 if half == halves - 1 else 0)
 
             def where(index, by):
                 return at(index, t + 1 + by, HALO + half * 8)
 
             for component in range(2):
                 kept = 1.0 - rates[component]
-                for direction, relaxed in equilibria(component, where, range(19)):
+                for direction, relaxed in equilibria(component, where, range(19), left_out):
                     if kept != 0.0:
                         relaxed = relaxed + kept * pop_at(component, direction, t, half)
                     bounced = pop_at(component, opposite(direction), t, half)
                     value = moved(direction, jnp.where(fluid, relaxed, bounced))
                     stream[where(19 * component + direction, 0), :] = value
-        return carry
-
-    def collide_outside(step):
-        for side in range(2):
-            row = first_row - 1 if side == 0 else last_row + 1
+
+    def collide_row(row):
+        for component in range(2):
+
+            def where(index, by):
+                return across(index, row, by)
+
+            for direction, relaxed in equilibria(component, where, range(19)):
+                place = where(19 * component + direction, 0)
+                stream[place, :] = stream[place, :] + moved(direction, relaxed)
+
+    def collide_outside_x(step, side):
+        row = first_row - 1 if side == 0 else last_row + 1
+        for component in range(2):
+
+            def where(index, by):
+                return across(index, row, by)
+
+            for direction, relaxed in equilibria(component, where, along_x[side]):
+                place = 5 * component + along_x[side].index(direction)
+                value = relaxed + recv_x[step, side, 9 + place].astype(f32)
+                stream[where(19 * component + direction, 0), :] = moved(direction, value)
+
+    def collide_outside_y(side, starts):
+        tile = 0 if side == 0 else tiles + 1
+        for start in starts:
             for component in range(2):
 
                 def where(index, by):
-                    return across(index, row, by)
-
-                for direction, relaxed in equilibria(component, where, along_x[side]):
-                    place = 5 * component + along_x[side].index(direction)
-                    value = relaxed + recv_x[step, side, 9 + place].astype(f32)
-                    stream[where(19 * component + direction, 0), :] = moved(direction, value)
-            tile = 0 if side == 0 else tiles + 1
-            for start in windows:
-                for component in range(2):
-
-                    def where(index, by):
-                        return off(index, min(max(tile + by, 0), tiles + 1), start)
-
-                    for direction, relaxed in equilibria(component, where, along_y[side]):
-                        place = 5 * component + along_y[side].index(direction)
-                        part = held_y[pl.ds((place * 2 + side) * rows + start, 8), :]
-                        value = moved(direction, relaxed + part)
-                        stream[where(19 * component + direction, 0), :] = value
+                    return off(index, min(max(tile + by, 0), tiles + 1), start)
+
+                for direction, relaxed in equilibria(component, where, along_y[side]):
+                    place = 5 * component + along_y[side].index(direction)
+                    part = held_y[pl.ds((place * 2 + side) * rows + start, 8), :]
+                    value = moved(direction, relaxed + part)
+                    stream[where(19 * component + direction, 0), :] = value
 
     def settle_step(last):
         target = out_ref if last else pops
@@ -477,52 +492,79 @@
                 inlet = jnp.logical_and(xglobal == planes_ref[0], fluid)
                 outlet = jnp.logical_and(xglobal == planes_ref[1], fluid)
                 fixed = jnp.logical_or(inlet, outlet)
-                densities = []
+                forced = [{}, {}]
                 for component in range(2):
-                    forced = {}
                     for weight in sorted(set(lattice_weights)):
                         values = [
-                            float(np.asarray(weight * level[component], jnp.bfloat16))
+                            float(np.asarray(weight * level[component], bf16))
                             for level in (INLET_DENSITY, OUTLET_DENSITY)
                         ]
-                        forced[weight] = jnp.where(inlet, values[0], values[1])
-                    total = None
-                    for direction in range(19):
-                        step_x, step_y, _ = velocities[direction]
-                        index = 19 * component + direction
-                        start = HALO + half * 8 - step_x
-                        value = stream[off(index, t + 1, start), :]
-                        if step_y == 1:
-                            value = jnp.where(low, stream[off(index, t, start), :], value)
-                        elif step_y == -1:
-                            value = jnp.where(low, value, stream[off(index, t + 2, start), :])
-                        value = jnp.where(fixed, forced[lattice_weights[direction]], value)
-                        narrow = value.astype(bf16)
-                        target[component, direction, half * 8 : half * 8 + 8, lanes] = narrow
-                        if not last:
-                            wide = narrow.astype(f32)
-                            total = wide if total is None else total + wide
-                    densities.append(total)
-                if not last:
-                    store_potential(t, half, densities)
+                        forced[component][weight] = jnp.where(inlet, values[0], values[1])
+
+                def get(component, direction):
+                    step_x, step_y, _ = velocities[direction]
+                    index = 19 * component + direction
+                    start = HALO + half * 8 - step_x
+                    value = stream[off(index, t + 1, start), :]
+                    if step_y == 1:
+                        value = jnp.where(low, stream[off(index, t, start), :], value)
+                    elif step_y == -1:
+                        value = jnp.where(low, value, stream[off(index, t + 2, start), :])
+                    value = jnp.where(fixed, forced[component][lattice_weights[direction]], value)
+                    narrow = value.astype(bf16)
+                    target[component, direction, half * 8 : half * 8 + 8, lanes] = narrow
+                    return narrow.astype(f32)
+
+                if last:
+                    for component in range(2):
+                        for direction in range(19):
+                            get(component, direction)
+                else:
+                    absorb(t, half, get)
             return carry
 
         lax.fori_loop(0, tiles, read, 0)
 
+    def clear(tile, carry):
+        for index in range(2):
+            for start in (0, HALO + size_x):
+                field[at(index, tile, start), :] = jnp.zeros((8, 128), f32)
+        return carry
+
+    def each_tile(first, last, step, work):
+        def body(k, carry):
+            work(first + k * step)
+            return carry
+
+        lax.fori_loop(0, (last - first) // step + 1, body, 0)
+
+    lax.fori_loop(0, tiles + 2, clear, 0)
     load_wall.wait()
-    lax.fori_loop(0, tiles, first_density, 0)
+    lax.fori_loop(0, tiles, first_absorb, 0)
     load_planes.wait()
-    lax.fori_loop(0, tiles, moments, 0)
     pl.semaphore_wait(barrier, len(targets))
+    sent = []
     for step in range(STEPS):
-        if step > 0:
-            lax.fori_loop(0, tiles, moments, 0)
         copies = send_edges(step)
-        receive_edges(step, copies)
-        lax.fori_loop(0, tiles + 2, spread_x, 0)
-        collide_outside(step)
-        lax.fori_loop(0, tiles, collide, 0)
+        sent += copies
+        each_tile(1, tiles, 1, lambda tile: spread_tile(tile, inner_windows))
+        each_tile(1, tiles - 2, 1, collide)
+        receive_faces(step, copies)
+        for row in (first_row - 1, first_row, last_row, last_row + 1):
+            spread_row(row)
+        each_tile(0, tiles + 1, tiles + 1, lambda tile: spread_tile(tile, inner_windows))
+        each_tile(0, tiles - 1, tiles - 1, collide)
+        for side in range(2):
+            collide_outside_y(side, middle_windows)
+        receive_corners(step, copies)
+        each_tile(0, tiles + 1, tiles + 1, lambda tile: spread_tile(tile, outer_windows))
+        for side in range(2):
+            collide_outside_y(side, outer_windows)
+            collide_outside_x(step, side)
+        each_tile(first_row, last_row, last_row - first_row, collide_row)
         settle_step(step == STEPS - 1)
+    for copy in sent:
+        copy.wait_send()
 
 
 def on_device(nx_devices, ny_devices, populations, wall_class, planes):

time: 44 us -> 39.6 us (0.900)
  Pallas kernels: 42.8 us -> 38 us
    pallas_call x1, Pallas kernels: 42.8 us -> 38 us  [on_device(): pl.pallas_call(functools.partial(kernel, nx_devices, ny_devices), out_sha...]
where the time goes in v3:
time: 39.6 us; the launch traced here: 39.1 us
  Pallas kernels  38 us (96%)
  local copies, waits for them, and re-layouts  1.04 us (3%)
    pallas_call x1, Pallas kernels, on_device(): pl.pallas_call(functools.partial(kernel, nx_devices, ny_devices), out_sha...  38 us
    unnamed x1, local copies, waits for them, and re-layouts  1.04 us

profile of v3, /device:TPU:7, one launch (start us, length us, event | category | flops | bytes accessed | tf_op | source)
XLA Modules:
  0.0 39.1 jit_solution(4599344083446072837)
XLA Ops:
  0.0 38.0 %shard_map.37 = bf16[2,19,16,1024]{3,2,1,0:T(8,128)(2,1)S(1)} custom-call(bf16[2,19,16,1024]{3,2,1,0:T(8,128)(2,1)} %pops_hbm.1, s32[16,1024]{1,0:T(8,128)} %wall_hbm.1, s32[2]{0:T(128)} %planes_hbm.1), custom_call_target="tpu_custom_call" | custom-call | tf_op jit(solution)/shard_map/pallas_call | solution.py:578
  38.0 1.0 %copy.5 = bf16[2,19,16,1024]{3,2,1,0:T(8,128)(2,1)} copy(bf16[2,19,16,1024]{3,2,1,0:T(8,128)(2,1)S(1)} %shard_map.37) | data formatting | bytes 2490368

commit v4 on v3

--- a/solution.py
+++ b/solution.py
@@ -44,6 +44,7 @@
 EDGES = ((0, 0), (0, 1), (1, 0), (1, 1))
 
 HALO = 8
+SPARE = 8
 
 
 def opposite(direction):
@@ -90,7 +91,7 @@
     size_x = pops.shape[2]
     tiles = pops.shape[3] // 128
     halves = size_x // 8
-    rows = size_x + 2 * HALO
+    rows = size_x + 2 * HALO + SPARE
     block = (tiles + 2) * rows
     first_row = HALO
     last_row = HALO + size_x - 1
@@ -103,8 +104,8 @@
     near_y = (lax.rem(gy + 1, ny_devices), lax.rem(gy + ny_devices - 1, ny_devices))
 
     barrier = pltpu.get_barrier_semaphore()
-    targets = [(near_x[0], gy), (near_x[1], gy), (gx, near_y[0]), (gx, near_y[1])]
-    targets += [(near_x[i], near_y[j]) for i, j in EDGES]
+    targets = [(near_x[i], near_y[j]) for i, j in EDGES]
+    targets += [(near_x[0], gy), (near_x[1], gy), (gx, near_y[0]), (gx, near_y[1])]
     for target in targets:
         pl.semaphore_signal(barrier, inc=1, device_id=target, device_id_type=MESH)
 
@@ -183,7 +184,7 @@
                 for toward, own, bounced in ((direction, one, two), (direction + 1, two, one)):
                     if toward in along_x[side]:
                         index = 5 * component + along_x[side].index(toward)
-                        start = pl.multiple_of((index * tiles + t) * size_x + half * 8, 8)
+                        start = pl.multiple_of((index * tiles + t) * (size_x + SPARE) + half * 8, 8)
                         held_x[pl.ds(start, 8), :] = kept_part(component, fluid, own, bounced)
             densities.append(total)
             momenta.append(parts)
@@ -213,7 +214,7 @@
         turned = roll(two, NZ)
         return jnp.where(low, turned, one) if side == 0 else jnp.where(low, one, turned)
 
-    def send_edges(step):
+    def pack_x(step):
         for side in range(2):
             row, inner = (last_row, last_row - 1) if side == 0 else (first_row, first_row + 1)
             for index in range(2):
@@ -222,9 +223,12 @@
             for index in range(5):
                 send_x[step, side, 4 + index] = aux[across(index, row), :].astype(bf16)
             for index in range(10):
-                start = index * tiles * size_x + row - HALO
-                part = held_x[pl.ds(start, tiles, stride=size_x), :]
+                start = index * tiles * (size_x + SPARE) + row - HALO
+                part = held_x[pl.ds(start, tiles, stride=size_x + SPARE), :]
                 send_x[step, side, 9 + index] = part.astype(bf16)
+
+    def pack_y(step):
+        for side in range(2):
             t = tiles - 1 if side == 0 else 0
             for half in range(halves):
                 place = t + 1, HALO + half * 8
@@ -245,26 +249,36 @@
                         for component in range(2)
                     ]
                     send_y[step, side, half, 5 + index] = pack(side, *parts).astype(bf16)
-        copies = []
-        for place, (i, j) in enumerate(EDGES):
-            source = send_y.at[step, j, halves - 1 if i == 0 else 0, pl.ds(0, EDGE_PARTS)]
-            copies.append((source, recv_c.at[step, place], (near_x[i], near_y[j])))
-        for side in range(2):
-            copies.append((send_x.at[step, side], recv_x.at[step, side], (near_x[side], gy)))
-            copies.append((send_y.at[step, side], recv_y.at[step, side], (gx, near_y[side])))
+
+    def start(step, base, copies):
         started = []
         for place, (source, target, device) in enumerate(copies):
             copy = pltpu.make_async_remote_copy(
                 src_ref=source,
                 dst_ref=target,
-                send_sem=send_sem.at[step, place],
-                recv_sem=recv_sem.at[step, place],
+                send_sem=send_sem.at[step, base + place],
+                recv_sem=recv_sem.at[step, base + place],
                 device_id=device,
                 device_id_type=MESH,
             )
             copy.start()
             started.append(copy)
         return started
+
+    def start_y(step):
+        copies = []
+        for place, (i, j) in enumerate(EDGES):
+            source = send_y.at[step, j, halves - 1 if i == 0 else 0, pl.ds(0, EDGE_PARTS)]
+            copies.append((source, recv_c.at[step, place], (near_x[i], near_y[j])))
+        for side in range(2):
+            copies.append((send_y.at[step, side], recv_y.at[step, side], (gx, near_y[side])))
+        return start(step, 0, copies)
+
+    def start_x(step):
+        copies = []
+        for side in range(2):
+            copies.append((send_x.at[step, side], recv_x.at[step, side], (near_x[side], gy)))
+        return start(step, len(EDGES) + 2, copies)
 
     def gain_of(component, source, density):
         return jnp.where(density == 0.0, 0.0, gains[component] * source / density)
@@ -306,11 +320,10 @@
                 base = ((5 * component + place) * 2 + side) * rows
                 held_y[pl.ds(base + start, 8), :] = part
 
-    def receive_faces(step, copies):
-        for copy in copies[len(EDGES) :]:
+    def receive_y(step, copies):
+        for copy in copies[len(EDGES) : len(EDGES) + 2]:
             copy.wait_recv()
         for side in range(2):
-            unpack_x(step, side)
             for half in range(halves):
                 unpack_y(
                     side,
@@ -318,6 +331,12 @@
                     HALO + half * 8,
                     face_order(side, half, halves),
                 )
+
+    def receive_x(step, copies):
+        for copy in copies[len(EDGES) + 2 :]:
+            copy.wait_recv()
+        for side in range(2):
+            unpack_x(step, side)
 
     def receive_corners(step, copies):
         for copy in copies[: len(EDGES)]:
@@ -481,10 +500,10 @@
                     value = moved(direction, relaxed + part)
                     stream[where(19 * component + direction, 0), :] = value
 
-    def settle_step(last):
+    def settle_step(last, first_tile, last_tile, stride):
         target = out_ref if last else pops
 
-        def read(t, carry):
+        def read(t):
             lanes = pl.ds(pl.multiple_of(t * 128, 128), 128)
             for half in range(halves):
                 fluid = wall_at(t, half) == 0
@@ -521,9 +540,8 @@
                             get(component, direction)
                 else:
                     absorb(t, half, get)
-            return carry
-
-        lax.fori_loop(0, tiles, read, 0)
+
+        each_tile(first_tile, last_tile, stride, read)
 
     def clear(tile, carry):
         for index in range(2):
@@ -542,27 +560,38 @@
     load_wall.wait()
     lax.fori_loop(0, tiles, first_absorb, 0)
     load_planes.wait()
+    pack_y(0)
+    pack_x(0)
     pl.semaphore_wait(barrier, len(targets))
+    copies = start_y(0) + start_x(0)
     sent = []
     for step in range(STEPS):
-        copies = send_edges(step)
         sent += copies
         each_tile(1, tiles, 1, lambda tile: spread_tile(tile, inner_windows))
         each_tile(1, tiles - 2, 1, collide)
-        receive_faces(step, copies)
+        receive_y(step, copies)
+        each_tile(0, tiles + 1, tiles + 1, lambda tile: spread_tile(tile, inner_windows))
+        each_tile(0, tiles - 1, tiles - 1, collide)
+        for side in range(2):
+            collide_outside_y(side, middle_windows)
+        receive_x(step, copies)
         for row in (first_row - 1, first_row, last_row, last_row + 1):
             spread_row(row)
-        each_tile(0, tiles + 1, tiles + 1, lambda tile: spread_tile(tile, inner_windows))
-        each_tile(0, tiles - 1, tiles - 1, collide)
-        for side in range(2):
-            collide_outside_y(side, middle_windows)
         receive_corners(step, copies)
         each_tile(0, tiles + 1, tiles + 1, lambda tile: spread_tile(tile, outer_windows))
         for side in range(2):
             collide_outside_y(side, outer_windows)
             collide_outside_x(step, side)
         each_tile(first_row, last_row, last_row - first_row, collide_row)
-        settle_step(step == STEPS - 1)
+        if step == STEPS - 1:
+            settle_step(True, 0, tiles - 1, 1)
+        else:
+            settle_step(False, 0, tiles - 1, tiles - 1)
+            pack_y(step + 1)
+            copies = start_y(step + 1)
+            settle_step(False, 1, tiles - 2, 1)
+            pack_x(step + 1)
+            copies = copies + start_x(step + 1)
     for copy in sent:
         copy.wait_send()
 
@@ -571,7 +600,7 @@
     size_x, width = populations.shape[2:]
     tiles = width // 128
     halves = size_x // 8
-    rows = size_x + 2 * HALO
+    rows = size_x + 2 * HALO + SPARE
     block = (tiles + 2) * rows
     bf16 = jnp.bfloat16
     f32 = jnp.float32
@@ -587,7 +616,7 @@
             pltpu.VMEM((2 * block, 128), f32),
             pltpu.VMEM((10 * block, 128), f32),
             pltpu.VMEM((7 * block, 128), f32),
-            pltpu.VMEM((10 * tiles * size_x, 128), f32),
+            pltpu.VMEM((10 * tiles * (size_x + SPARE), 128), f32),
             pltpu.VMEM((20 * rows, 128), f32),
             pltpu.VMEM((38 * block, 128), f32),
             pltpu.VMEM((STEPS, 2, X_PARTS, tiles, 128), bf16),

time: 39.6 us -> 37.3 us (0.942)
  Pallas kernels: 38 us -> 35.9 us
    pallas_call x1, Pallas kernels: 38 us -> 35.9 us  [on_device(): pl.pallas_call(functools.partial(kernel, nx_devices, ny_devices), out_sha...]
where the time goes in v4:
time: 37.3 us; the launch traced here: 36.9 us
  Pallas kernels  35.9 us (96%)
  local copies, waits for them, and re-layouts  1.04 us (3%)
    pallas_call x1, Pallas kernels, on_device(): pl.pallas_call(functools.partial(kernel, nx_devices, ny_devices), out_sha...  35.9 us
    unnamed x1, local copies, waits for them, and re-layouts  1.04 us

profile of v4, /device:TPU:7, one launch (start us, length us, event | category | flops | bytes accessed | tf_op | source)
XLA Modules:
  0.0 36.9 jit_solution(7990182703683518394)
XLA Ops:
  0.0 35.9 %shard_map.37 = bf16[2,19,16,1024]{3,2,1,0:T(8,128)(2,1)S(1)} custom-call(bf16[2,19,16,1024]{3,2,1,0:T(8,128)(2,1)} %pops_hbm.1, s32[16,1024]{1,0:T(8,128)} %wall_hbm.1, s32[2]{0:T(128)} %planes_hbm.1), custom_call_target="tpu_custom_call" | custom-call | tf_op jit(solution)/shard_map/pallas_call | solution.py:607
  35.9 1.0 %copy.5 = bf16[2,19,16,1024]{3,2,1,0:T(8,128)(2,1)} copy(bf16[2,19,16,1024]{3,2,1,0:T(8,128)(2,1)S(1)} %shard_map.37) | data formatting | bytes 2490368

commit v5 on v4

--- a/solution.py
+++ b/solution.py
@@ -368,7 +368,7 @@
 
     def spread_tile(tile, starts):
         for start in starts:
-            spread_at(lambda index, by: off(index, tile, start + by))
+            spread_at(lambda index, by: (off if (start + by) % 8 else at)(index, tile, start + by))
 
     def spread_row(row):
         spread_at(lambda index, by: across(index, row + by))
@@ -524,11 +524,12 @@
                     step_x, step_y, _ = velocities[direction]
                     index = 19 * component + direction
                     start = HALO + half * 8 - step_x
-                    value = stream[off(index, t + 1, start), :]
+                    rows_of = off if step_x else at
+                    value = stream[rows_of(index, t + 1, start), :]
                     if step_y == 1:
-                        value = jnp.where(low, stream[off(index, t, start), :], value)
+                        value = jnp.where(low, stream[rows_of(index, t, start), :], value)
                     elif step_y == -1:
-                        value = jnp.where(low, value, stream[off(index, t + 2, start), :])
+                        value = jnp.where(low, value, stream[rows_of(index, t + 2, start), :])
                     value = jnp.where(fixed, forced[component][lattice_weights[direction]], value)
                     narrow = value.astype(bf16)
                     target[component, direction, half * 8 : half * 8 + 8, lanes] = narrow

time: 37.3 us -> 37.3 us (level)
  no operation moved by 1% of the time
where the time goes in v5:
time: 37.3 us; the launch traced here: 36.9 us
  Pallas kernels  35.9 us (96%)
  local copies, waits for them, and re-layouts  1.04 us (3%)
    pallas_call x1, Pallas kernels, on_device(): pl.pallas_call(functools.partial(kernel, nx_devices, ny_devices), out_sha...  35.9 us
    unnamed x1, local copies, waits for them, and re-layouts  1.04 us

profile of v5, /device:TPU:7, one launch (start us, length us, event | category | flops | bytes accessed | tf_op | source)
XLA Modules:
  0.0 36.9 jit_solution(7990182703683518394)
XLA Ops:
  0.0 35.9 %shard_map.37 = bf16[2,19,16,1024]{3,2,1,0:T(8,128)(2,1)S(1)} custom-call(bf16[2,19,16,1024]{3,2,1,0:T(8,128)(2,1)} %pops_hbm.1, s32[16,1024]{1,0:T(8,128)} %wall_hbm.1, s32[2]{0:T(128)} %planes_hbm.1), custom_call_target="tpu_custom_call" | custom-call | tf_op jit(solution)/shard_map/pallas_call | solution.py:608
  35.9 1.0 %copy.5 = bf16[2,19,16,1024]{3,2,1,0:T(8,128)(2,1)} copy(bf16[2,19,16,1024]{3,2,1,0:T(8,128)(2,1)S(1)} %shard_map.37) | data formatting | bytes 2490368
